TPU v7x, 32 devices: a whole 2x2x4 slice. The times are simulated.
32 devices in a mesh: outer: 8 (over z, x), inner: 4 (over y, core).
Axes of the slice: x: 2, y: 2, z: 4, core: 2. Of those that a mesh axis runs over, the one named last changes fastest.
Arguments:
- user_factors: float32 [16384, 256], P(('outer', 'inner')), may hold values from -0.3 to 0.3
- item_factors: float32 [16384, 256], P(('outer', 'inner')), may hold values from -0.3 to 0.3
- ratings: bfloat16 [16384, 8, 512], P(('outer', 'inner')), may hold values from -6 to 6
- weights: bfloat16 [16384, 8, 512], P(('outer', 'inner')), may hold values from 0 to 2, as said below
- tile_list: int32 [32, 8, 4], P(('outer', 'inner')), may hold values from 0 to 3, as said below
- tile_count: int32 [32, 8], P(('outer', 'inner')), may hold values from 1 to 4, as said below
Outputs:
- users_out: float32 [16384, 256], P(('outer', 'inner'))
- items_out: float32 [16384, 256], P(('outer', 'inner'))
Inputs may be any that keep to these rules, and one draw needn't show every extreme that they name: Every row tile_list[d,k,:] names each of 0 to 3 once. `tile_count`: in every draw some device lists all 4 tiles in some stratum. `weights`: zero outside the listed tiles and at unobserved entries; elsewhere between 0.5 and 2.
All inputs are finite; a program needn't handle non-finite values.
Results may differ from a plain program's by a relative error of at most 0.003.
Values sent between devices are 32-bit elements; how exact they have to be, the bound alone decides.
No kernel may reach another device: no remote copies, remote signals or barrier semaphores. Data moves between devices by JAX's collectives and lax.ppermute only.
A program may use at most 64 MiB of HBM per device.

v0:
```python
import jax
import jax.numpy as jnp
from jax import lax
from jax.experimental import pallas as pl
from jax.experimental.pallas import tpu as pltpu
from jax.sharding import PartitionSpec as P


S_OUT = 2
S_IN = 4
SHARES = (1, 1, 1, 1)
LATER = ((2, 3, 4), (5, 6, 7))
CHUNK = 32
GROUP = 128
LANES = 128

learn_rate = 0.015
ridge_weight = 0.05


VMEM = pl.BlockSpec(memory_space=pltpu.VMEM)
HBM = pl.BlockSpec(memory_space=pltpu.HBM)
LIMIT = 24 * 1024 * 1024
RANK = (((1,), (1,)), ((), ()))
USERS = (((0,), (0,)), ((), ()))
f32 = jnp.float32
bf16 = jnp.bfloat16


def from_behind(value, axis, steps):
    count = lax.axis_size(axis)
    pairs = [(source, (source + steps) % count) for source in range(count)]
    return lax.ppermute(value, axis, pairs)


def move_items(item_rows, outer_step, inner_step):
    if inner_step < S_IN - 1:
        return from_behind(item_rows, "inner", 1)
    if outer_step < S_OUT - 1:
        return from_behind(item_rows, "outer", 1)
    return item_rows


def call(kernel, out_shape, in_specs, out_specs, flops, scratch=()):
    return pl.pallas_call(
        kernel,
        out_shape=out_shape,
        in_specs=in_specs,
        out_specs=out_specs,
        scratch_shapes=scratch,
        compiler_params=pltpu.CompilerParams(vmem_limit_bytes=LIMIT),
        cost_estimate=pl.CostEstimate(flops=flops, bytes_accessed=1024, transcendentals=0),
    )


def cut(items):
    unit = items // sum(SHARES)
    return [unit * sum(SHARES[:j]) for j in range(len(SHARES))], [unit * share for share in SHARES]


def hbm(value):
    return pltpu.with_memory_space_constraint(value, pltpu.HBM)


def load(user_factors, item_factors, ratings, weights, tile_list, tile_count):
    users, strata, items = ratings.shape
    rank = item_factors.shape[1]
    tiles = tile_list.shape[2]
    width = items // tiles
    starts, sizes = cut(items)
    count = len(sizes)
    blocks = items // LANES

    def view(table):
        table = table.reshape(users, strata, blocks, LANES).transpose(0, 2, 1, 3)
        return table.reshape(users, blocks, strata // 2, 2, LANES)

    def kernel(
        list_hbm, count_hbm, user_hbm, item_hbm, rating_hbm, weight_hbm,
        rating_out, weight_out, mask_out, user_out, half_out, *refs,
    ):
        pieces, (raw, lists, counts, sems, small) = refs[:count], refs[count:]
        tables = [
            pltpu.make_async_copy(list_hbm, lists, small.at[0]),
            pltpu.make_async_copy(count_hbm, counts, small.at[1]),
        ]
        factors = [pltpu.make_async_copy(user_hbm, user_out, small.at[2])] + [
            pltpu.make_async_copy(item_hbm.at[pl.ds(starts[j], sizes[j])], pieces[j], small.at[3 + j])
            for j in range(count)
        ]
        copies = [
            [
                pltpu.make_async_copy(source.at[:, block, 0], raw.at[side, block], sems.at[side, block])
                for block in range(blocks)
            ]
            for side, source in enumerate((rating_hbm, weight_hbm))
        ]
        for copy in tables + copies[0] + copies[1] + factors:
            copy.start()
        target = lax.broadcasted_iota(jnp.int32, (2 * GROUP, 2 * GROUP), 0)
        source = lax.broadcasted_iota(jnp.int32, (2 * GROUP, 2 * GROUP), 1)
        wanted = (target % GROUP) * 2 + target // GROUP
        pick = jnp.where(source == wanted, 1.0, 0.0).astype(bf16)
        for copy in tables:
            copy.wait()
        for stratum in range(strata):
            for tile in range(tiles):
                listed = jnp.float32(0.0)
                for slot in range(tiles):
                    hit = (lists[slot, stratum] == tile) & (slot < counts[0, stratum])
                    listed = jnp.where(hit, 1.0, listed)
                mask_out[stratum : stratum + 1, tile * width : (tile + 1) * width] = jnp.full((1, width), listed)
        for side, out in enumerate((rating_out, weight_out)):
            for copy in copies[side]:
                copy.wait()
            for block in range(blocks):
                pairs = raw.at[side, block].reshape(2 * users, LANES)
                cols = slice(block * LANES, (block + 1) * LANES)
                for first in range(0, users, GROUP):
                    rows = jnp.dot(pick, pairs[2 * first : 2 * (first + GROUP), :], preferred_element_type=f32)
                    for stratum in range(2):
                        part = rows[stratum * GROUP : (stratum + 1) * GROUP]
                        if side == 1:
                            part = part * mask_out[stratum : stratum + 1, cols]
                        out[stratum, first : first + GROUP, cols] = part.astype(bf16)
        for copy in factors:
            copy.wait()
        half_out[...] = user_out[...].astype(bf16)

    table = jax.ShapeDtypeStruct((2, users, items), bf16)
    outs = call(
        kernel,
        (
            table,
            table,
            jax.ShapeDtypeStruct((strata, items), f32),
            jax.ShapeDtypeStruct((users, rank), f32),
            jax.ShapeDtypeStruct((users, rank), bf16),
            *[jax.ShapeDtypeStruct((size, rank), f32) for size in sizes],
        ),
        [HBM] * 6,
        (VMEM,) * (5 + count),
        8 * users * items * GROUP,
        [
            pltpu.VMEM((2, blocks, users, 2, LANES), bf16),
            pltpu.SMEM((tiles, strata), jnp.int32),
            pltpu.SMEM((1, strata), jnp.int32),
            pltpu.SemaphoreType.DMA((2, blocks)),
            pltpu.SemaphoreType.DMA((3 + count,)),
        ],
    )(
        hbm(tile_list[0].T), hbm(tile_count), hbm(user_factors), hbm(item_factors),
        hbm(view(ratings)), hbm(view(weights)),
    )
    return *outs[:5], list(outs[5:])


def sort_strata(chosen, ratings, weights, mask):
    users, strata, items = ratings.shape
    rows = CHUNK * strata
    kept = len(chosen)

    def kernel(rating_ref, weight_ref, mask_ref, rating_out, weight_out):
        target = lax.broadcasted_iota(jnp.int32, (CHUNK * kept, rows), 0)
        source = lax.broadcasted_iota(jnp.int32, (CHUNK * kept, rows), 1)
        wanted = (target % CHUNK) * strata + target // CHUNK + chosen[0]
        pick = jnp.where(source == wanted, 1.0, 0.0).astype(bf16)
        for first in range(0, users, CHUNK):
            mine = slice(first * strata, first * strata + rows)
            into = slice(first, first + CHUNK)
            rating = jnp.dot(pick, rating_ref[mine, :], preferred_element_type=f32)
            weight = jnp.dot(pick, weight_ref[mine, :], preferred_element_type=f32)
            for index, stratum in enumerate(chosen):
                part = slice(index * CHUNK, (index + 1) * CHUNK)
                rating_out[index, into, :] = rating[part].astype(bf16)
                weight_out[index, into, :] = (weight[part] * mask_ref[stratum : stratum + 1, :]).astype(bf16)

    table = jax.ShapeDtypeStruct((kept, users, items), bf16)
    return call(
        kernel, (table, table), [VMEM] * 3, (VMEM, VMEM), 4 * kept * users * items * rows
    )(ratings.reshape(users * strata, items), weights.reshape(users * strata, items), mask)


def piece_step(user_half, rows, rating_ref, weight_ref, stratum, cols):
    predicted = lax.dot_general(user_half, rows.astype(bf16), RANK, preferred_element_type=f32)
    rating = rating_ref[stratum, :, cols].astype(f32)
    weight = weight_ref[stratum, :, cols].astype(f32)
    residual = (weight * (predicted - rating)).astype(bf16)
    grad = lax.dot_general(residual, user_half, USERS, preferred_element_type=f32)
    return residual, rows - learn_rate * (grad + ridge_weight * rows)


def users_grad(residual, rows):
    return jnp.dot(residual, rows.astype(bf16), preferred_element_type=f32)


def first_piece(stratum, cols, user_half, piece, ratings, weights):
    def kernel(half_ref, piece_ref, rating_ref, weight_ref, new_ref, residual_ref):
        residual_ref[...], new_ref[...] = piece_step(
            half_ref[...], piece_ref[...], rating_ref, weight_ref, stratum, cols
        )

    users = user_half.shape[0]
    m, rank = piece.shape
    return call(
        kernel,
        (jax.ShapeDtypeStruct((m, rank), f32), jax.ShapeDtypeStruct((users, m), bf16)),
        [VMEM] * 4,
        (VMEM, VMEM),
        4 * users * m * rank,
    )(user_half, piece, ratings, weights)


def middle_piece(stratum, cols, user_rows, user_half, piece, ratings, weights, earlier):
    def kernel(user_ref, half_ref, piece_ref, rating_ref, weight_ref, *refs):
        earlier_refs, (new_ref, grad_ref) = refs[:-2], refs[-2:]
        rows = piece_ref[...]
        residual, new_ref[...] = piece_step(half_ref[...], rows, rating_ref, weight_ref, stratum, cols)
        if len(earlier_refs) == 2:
            grad = ridge_weight * user_ref[...] + users_grad(earlier_refs[1][...], earlier_refs[0][...])
        else:
            grad = earlier_refs[0][...]
        grad_ref[...] = grad + users_grad(residual, rows)

    users = user_half.shape[0]
    m, rank = piece.shape
    return call(
        kernel,
        (jax.ShapeDtypeStruct((m, rank), f32), jax.ShapeDtypeStruct((users, rank), f32)),
        [VMEM] * (5 + len(earlier)),
        (VMEM, VMEM),
        8 * users * m * rank,
    )(user_rows, user_half, piece, ratings, weights, *earlier)


def last_piece(stratum, cols, user_rows, user_half, grad, piece, ratings, weights):
    def kernel(user_ref, half_ref, grad_ref, piece_ref, rating_ref, weight_ref, new_ref, user_out, half_out):
        rows = piece_ref[...]
        residual, new_ref[...] = piece_step(half_ref[...], rows, rating_ref, weight_ref, stratum, cols)
        user = user_ref[...] - learn_rate * (grad_ref[...] + users_grad(residual, rows))
        user_out[...] = user
        half_out[...] = user.astype(bf16)

    users = user_half.shape[0]
    m, rank = piece.shape
    return call(
        kernel,
        (
            jax.ShapeDtypeStruct((m, rank), f32),
            jax.ShapeDtypeStruct((users, rank), f32),
            jax.ShapeDtypeStruct((users, rank), bf16),
        ),
        [VMEM] * 6,
        (VMEM,) * 3,
        6 * users * m * rank,
    )(user_rows, user_half, grad, piece, ratings, weights)


def finish(stratum, cols, user_rows, user_half, grad, piece, ratings, weights, news):
    m, rank = piece.shape
    users = user_rows.shape[0]
    done = len(news)

    def kernel(user_ref, half_ref, grad_ref, piece_ref, rating_ref, weight_ref, *refs):
        new_refs, (users_out, items_out, last_items, last_users, sems) = refs[:done], refs[done:]
        copies = []

        def write(source, target):
            copies.append(pltpu.make_async_copy(source, target, sems.at[len(copies)]))
            copies[-1].start()

        start = 0
        for new_ref in new_refs:
            write(new_ref, items_out.at[pl.ds(start, new_ref.shape[0])])
            start += new_ref.shape[0]
        rows = piece_ref[...]
        residual, new_rows = piece_step(half_ref[...], rows, rating_ref, weight_ref, stratum, cols)
        last_users[...] = user_ref[...] - learn_rate * (grad_ref[...] + users_grad(residual, rows))
        write(last_users, users_out)
        last_items[...] = new_rows
        write(last_items, items_out.at[pl.ds(start, m)])
        for copy in copies:
            copy.wait()

    items = m + sum(new.shape[0] for new in news)
    return call(
        kernel,
        (jax.ShapeDtypeStruct((users, rank), f32), jax.ShapeDtypeStruct((items, rank), f32)),
        [VMEM] * (6 + done),
        (HBM, HBM),
        6 * users * m * rank,
        [
            pltpu.VMEM((m, rank), f32),
            pltpu.VMEM((users, rank), f32),
            pltpu.SemaphoreType.DMA((done + 2,)),
        ],
    )(user_rows, user_half, grad, piece, ratings, weights, *news)


def local(user_factors, item_factors, ratings, weights, tile_list, tile_count):
    starts, sizes = cut(item_factors.shape[0])
    cols = [slice(start, start + size) for start, size in zip(starts, sizes)]
    last = len(sizes) - 1
    rating_01, weight_01, mask, user_rows, user_half, pieces = load(
        user_factors, item_factors, ratings, weights, tile_list, tile_count
    )
    tables = [(0, rating_01, weight_01), (1, rating_01, weight_01)]
    for chosen in LATER:
        sorted_ratings, sorted_weights = sort_strata(chosen, ratings, weights, mask)
        tables.extend((index, sorted_ratings, sorted_weights) for index in range(len(chosen)))
    for outer_step in range(S_OUT):
        for inner_step in range(S_IN):
            stratum = outer_step * S_IN + inner_step
            row, rating, weight = tables[stratum]

            def move(new):
                return move_items(new, outer_step, inner_step)

            new, residual = first_piece(row, cols[0], user_half, pieces[0], rating, weight)
            news = [move(new)]
            earlier = (pieces[0], residual)
            for j in range(1, last):
                new, grad = middle_piece(row, cols[j], user_rows, user_half, pieces[j], rating, weight, earlier)
                news.append(move(new))
                earlier = (grad,)
            if stratum == S_OUT * S_IN - 1:
                return finish(
                    row, cols[last], user_rows, user_half, grad, pieces[last], rating, weight, news
                )
            new, user_rows, user_half = last_piece(
                row, cols[last], user_rows, user_half, grad, pieces[last], rating, weight
            )
            news.append(move(new))
            pieces = news


def solution(mesh):
    in_specs = (
        P(("outer", "inner"), None),
        P(("outer", "inner"), None),
        P(("outer", "inner"), None, None),
        P(("outer", "inner"), None, None),
        P(("outer", "inner"), None, None),
        P(("outer", "inner"), None),
    )
    out_specs = (P(("outer", "inner"), None), P(("outer", "inner"), None))

    return jax.shard_map(local, mesh=mesh, in_specs=in_specs, out_specs=out_specs, check_vma=False)
```

profile of v0, /device:TPU:0, one launch (start us, length us, event | category | flops | bytes accessed | tf_op | source)
XLA Modules:
  0.0 58.8 jit_solution(14383681305280836419)
XLA Ops:
  0.6 3.1 %shard_map.77 = (bf16[2,512,512]{2,1,0:T(8,128)(2,1)S(1)}, bf16[2,512,512]{2,1,0:T(8,128)(2,1)S(1)}, f32[8,512]{1,0:T(8,128)S(1)}, f32[512,256]{1,0:T(8,128)S(1)...) custom-call(s32[4,8]{1,0:T(4,128)} %bitcast.21, ...), custom_call_target="tpu_custom_call" | custom-call | flops 268435456 | bytes 1024 | tf_op jit(solution)/shard_map/pallas_call | solution.py:131
  4.7 0.7 %shard_map.79 = (f32[128,256]{1,0:T(8,128)S(1)}, f32[512,256]{1,0:T(8,128)S(1)}) custom-call(f32[512,256]{1,0:T(8,128)S(1)} %get-tuple-element.84.user_ref, bf16[512,256]{1,0:T(8,128)(2,1)S(1)} %get-tuple-element.85.half_ref, f32[128,256]{1,0:T(8,128)S(1)} %get-tuple-element.89.piece_ref, bf16[2,512,512]{2,1,0:T(8,128)(2,1)S(1)} %get-tuple-element.87.rating_ref, ...), custom_call_target="tpu_custom_call" | custom-call | flops 134217728 | bytes 1024 | tf_op jit(solution)/shard_map/pallas_call | solution.py:227
  5.4 2.7 %collective-permute-start.1 = (f32[128,256]{1,0:T(8,128)S(1)}, f32[128,256]{1,0:T(8,128)S(1)}, u32[]{:S(2)}, u32[]{:S(2)}) collective-permute-start(f32[128,256]{1,0:T(8,128)S(1)} %get-tuple-element.98), channel_id=1, source_target_pairs={{0,1},{1,2},{2,3},{3,0},{4,5},{5,6},{6,7},{7,4},{8,9},{9,10},{10,1... | collective-permute-start | bytes 393224 | tf_op jit(solution)/shard_map/ppermute | solution.py:33
  10.0 0.7 %collective-permute-done.1.piece_ref = f32[128,256]{1,0:T(8,128)S(1)} collective-permute-done((f32[128,256]{1,0:T(8,128)S(1)}, f32[128,256]{1,0:T(8,128)S(1)}, u32[]{:S(2)}, u32[]{:S(2)}) %collective-permute-start.1) | collective-permute-done | bytes 131104 | tf_op jit(solution)/shard_map/ppermute | solution.py:33
  10.7 0.7 %shard_map.83 = (f32[128,256]{1,0:T(8,128)S(1)}, f32[512,256]{1,0:T(8,128)S(1)}) custom-call(f32[512,256]{1,0:T(8,128)S(1)} %get-tuple-element.95.user_ref, bf16[512,256]{1,0:T(8,128)(2,1)S(1)} %get-tuple-element.96.half_ref, f32[128,256]{1,0:T(8,128)S(1)} %collective-permute-done.1.piece_ref, bf16[2,512,512]{2,1,0:T(8,128)(2,1)S(1)} %get-tuple-element.87.rating_ref, ...), custom_call_target="tpu_custom_call" | custom-call | flops 134217728 | bytes 1024 | tf_op jit(solution)/shard_map/pallas_call | solution.py:227
  11.4 1.6 %collective-permute-start.5 = (f32[128,256]{1,0:T(8,128)S(1)}, f32[128,256]{1,0:T(8,128)S(1)}, u32[]{:S(2)}, u32[]{:S(2)}) collective-permute-start(f32[128,256]{1,0:T(8,128)S(1)} %get-tuple-element.110), channel_id=1, source_target_pairs={{0,1},{1,2},{2,3},{3,0},{4,5},{5,6},{6,7},{7,4},{8,9},{9,10},{10,1... | collective-permute-start | bytes 393224 | tf_op jit(solution)/shard_map/ppermute | solution.py:33
  13.8 0.8 %collective-permute-start.4 = (f32[128,256]{1,0:T(8,128)S(1)}, f32[128,256]{1,0:T(8,128)S(1)}, u32[]{:S(2)}, u32[]{:S(2)}) collective-permute-start(f32[128,256]{1,0:T(8,128)S(1)} %get-tuple-element.106), channel_id=1, source_target_pairs={{0,1},{1,2},{2,3},{3,0},{4,5},{5,6},{6,7},{7,4},{8,9},{9,10},{10,1... | collective-permute-start | bytes 393224 | tf_op jit(solution)/shard_map/ppermute | solution.py:33
  15.2 0.7 %collective-permute-start.7 = (f32[128,256]{1,0:T(8,128)S(1)}, f32[128,256]{1,0:T(8,128)S(1)}, u32[]{:S(2)}, u32[]{:S(2)}) collective-permute-start(f32[128,256]{1,0:T(8,128)S(1)} %get-tuple-element.115), channel_id=1, source_target_pairs={{0,1},{1,2},{2,3},{3,0},{4,5},{5,6},{6,7},{7,4},{8,9},{9,10},{10,1... | collective-permute-start | bytes 393224 | tf_op jit(solution)/shard_map/ppermute | solution.py:33
  15.9 1.5 %shard_map.86 = (bf16[3,512,512]{2,1,0:T(8,128)(2,1)S(1)}, bf16[3,512,512]{2,1,0:T(8,128)(2,1)S(1)}) custom-call(bf16[4096,512]{1,0:T(8,128)(2,1)S(1)} %bitcast.16, bf16[4096,512]{1,0:T(8,128)(2,1)S(1)} %bitcast.19, f32[8,512]{1,0:T(8,128)S(1)} %get-tuple-element.107.mask_ref), custom_call_target="tpu_custom_call" | custom-call | flops 805306368 | bytes 1024 | tf_op jit(solution)/shard_map/pallas_call | solution.py:179
  17.9 0.8 %collective-permute-start.10 = (f32[128,256]{1,0:T(8,128)S(1)}, f32[128,256]{1,0:T(8,128)S(1)}, u32[]{:S(2)}, u32[]{:S(2)}) collective-permute-start(f32[128,256]{1,0:T(8,128)S(1)} %get-tuple-element.120), channel_id=1, source_target_pairs={{0,1},{1,2},{2,3},{3,0},{4,5},{5,6},{6,7},{7,4},{8,9},{9,10},{10,1... | collective-permute-start | bytes 393224 | tf_op jit(solution)/shard_map/ppermute | solution.py:33
  18.6 0.7 %shard_map.88 = (f32[128,256]{1,0:T(8,128)S(1)}, f32[512,256]{1,0:T(8,128)S(1)}) custom-call(f32[512,256]{1,0:T(8,128)S(1)} %get-tuple-element.104.user_ref, bf16[512,256]{1,0:T(8,128)(2,1)S(1)} %get-tuple-element.105.half_ref, f32[128,256]{1,0:T(8,128)S(1)} %collective-permute-done.5.piece_ref, bf16[3,512,512]{2,1,0:T(8,128)(2,1)S(1)} %get-tuple-element.108.rating_ref, ...), custom_call_target="tpu_custom_call" | custom-call | flops 134217728 | bytes 1024 | tf_op jit(solution)/shard_map/pallas_call | solution.py:227
  21.5 0.7 %collective-permute-start.11 = (f32[128,256]{1,0:T(8,128)S(1)}, f32[128,256]{1,0:T(8,128)S(1)}, u32[]{:S(2)}, u32[]{:S(2)}) collective-permute-start(f32[128,256]{1,0:T(8,128)S(1)} %get-tuple-element.124), channel_id=1, source_target_pairs={{0,1},{1,2},{2,3},{3,0},{4,5},{5,6},{6,7},{7,4},{8,9},{9,10},{10,1... | collective-permute-start | bytes 393224 | tf_op jit(solution)/shard_map/ppermute | solution.py:33
  22.8 1.5 %collective-permute-start.14 = (f32[128,256]{1,0:T(8,128)S(1)}, f32[128,256]{1,0:T(8,128)S(1)}, u32[]{:S(2)}, u32[]{:S(2)}) collective-permute-start(f32[128,256]{1,0:T(8,128)S(1)} %get-tuple-element.129), channel_id=1, source_target_pairs={{0,4},{4,8},{8,12},{12,16},{16,20},{20,24},{24,28},{28,0},{1,5},{5... | collective-permute-start | bytes 393224 | tf_op jit(solution)/shard_map/ppermute | solution.py:33
  25.0 1.6 %collective-permute-start.13 = (f32[128,256]{1,0:T(8,128)S(1)}, f32[128,256]{1,0:T(8,128)S(1)}, u32[]{:S(2)}, u32[]{:S(2)}) collective-permute-start(f32[128,256]{1,0:T(8,128)S(1)} %get-tuple-element.128), channel_id=1, source_target_pairs={{0,4},{4,8},{8,12},{12,16},{16,20},{20,24},{24,28},{28,0},{1,5},{5... | collective-permute-start | bytes 393224 | tf_op jit(solution)/shard_map/ppermute | solution.py:33
  27.2 1.5 %collective-permute-start.12 = (f32[128,256]{1,0:T(8,128)S(1)}, f32[128,256]{1,0:T(8,128)S(1)}, u32[]{:S(2)}, u32[]{:S(2)}) collective-permute-start(f32[128,256]{1,0:T(8,128)S(1)} %get-tuple-element.127), channel_id=1, source_target_pairs={{0,4},{4,8},{8,12},{12,16},{16,20},{20,24},{24,28},{28,0},{1,5},{5... | collective-permute-start | bytes 393224 | tf_op jit(solution)/shard_map/ppermute | solution.py:33
  29.4 1.6 %collective-permute-start.15 = (f32[128,256]{1,0:T(8,128)S(1)}, f32[128,256]{1,0:T(8,128)S(1)}, u32[]{:S(2)}, u32[]{:S(2)}) collective-permute-start(f32[128,256]{1,0:T(8,128)S(1)} %get-tuple-element.133), channel_id=1, source_target_pairs={{0,4},{4,8},{8,12},{12,16},{16,20},{20,24},{24,28},{28,0},{1,5},{5... | collective-permute-start | bytes 393224 | tf_op jit(solution)/shard_map/ppermute | solution.py:33
  31.0 0.9 %collective-permute-done.14.piece_ref.refs_0_ = f32[128,256]{1,0:T(8,128)S(1)} collective-permute-done((f32[128,256]{1,0:T(8,128)S(1)}, f32[128,256]{1,0:T(8,128)S(1)}, u32[]{:S(2)}, u32[]{:S(2)}) %collective-permute-start.14) | collective-permute-done | bytes 131104 | tf_op jit(solution)/shard_map/ppermute | solution.py:33
  32.4 2.3 %collective-permute-done.13.piece_ref = f32[128,256]{1,0:T(8,128)S(1)} collective-permute-done((f32[128,256]{1,0:T(8,128)S(1)}, f32[128,256]{1,0:T(8,128)S(1)}, u32[]{:S(2)}, u32[]{:S(2)}) %collective-permute-start.13) | collective-permute-done | bytes 131104 | tf_op jit(solution)/shard_map/ppermute | solution.py:33
  35.6 1.9 %collective-permute-done.12.piece_ref = f32[128,256]{1,0:T(8,128)S(1)} collective-permute-done((f32[128,256]{1,0:T(8,128)S(1)}, f32[128,256]{1,0:T(8,128)S(1)}, u32[]{:S(2)}, u32[]{:S(2)}) %collective-permute-start.12) | collective-permute-done | bytes 131104 | tf_op jit(solution)/shard_map/ppermute | solution.py:33
  38.2 1.9 %collective-permute-done.15.piece_ref = f32[128,256]{1,0:T(8,128)S(1)} collective-permute-done((f32[128,256]{1,0:T(8,128)S(1)}, f32[128,256]{1,0:T(8,128)S(1)}, u32[]{:S(2)}, u32[]{:S(2)}) %collective-permute-start.15) | collective-permute-done | bytes 131104 | tf_op jit(solution)/shard_map/ppermute | solution.py:33
  40.8 1.5 %shard_map.99 = (bf16[3,512,512]{2,1,0:T(8,128)(2,1)S(1)}, bf16[3,512,512]{2,1,0:T(8,128)(2,1)S(1)}) custom-call(bf16[4096,512]{1,0:T(8,128)(2,1)S(1)} %bitcast.17, bf16[4096,512]{1,0:T(8,128)(2,1)S(1)} %bitcast.20, f32[8,512]{1,0:T(8,128)S(1)} %get-tuple-element.107.mask_ref), custom_call_target="tpu_custom_call" | custom-call | flops 805306368 | bytes 1024 | tf_op jit(solution)/shard_map/pallas_call | solution.py:179
  42.7 0.9 %collective-permute-start.22 = (f32[128,256]{1,0:T(8,128)S(1)}, f32[128,256]{1,0:T(8,128)S(1)}, u32[]{:S(2)}, u32[]{:S(2)}) collective-permute-start(f32[128,256]{1,0:T(8,128)S(1)} %get-tuple-element.149), channel_id=1, source_target_pairs={{0,1},{1,2},{2,3},{3,0},{4,5},{5,6},{6,7},{7,4},{8,9},{9,10},{10,1... | collective-permute-start | bytes 393224 | tf_op jit(solution)/shard_map/ppermute | solution.py:33
  43.6 0.7 %shard_map.101 = (f32[128,256]{1,0:T(8,128)S(1)}, f32[512,256]{1,0:T(8,128)S(1)}) custom-call(f32[512,256]{1,0:T(8,128)S(1)} %get-tuple-element.134.user_ref, bf16[512,256]{1,0:T(8,128)(2,1)S(1)} %get-tuple-element.135.half_ref, f32[128,256]{1,0:T(8,128)S(1)} %collective-permute-done.17.piece_ref, bf16[3,512,512]{2,1,0:T(8,128)(2,1)S(1)} %get-tuple-element.137.rating_ref, ...), custom_call_target="tpu_custom_call" | custom-call | flops 134217728 | bytes 1024 | tf_op jit(solution)/shard_map/pallas_call | solution.py:227
  45.0 1.4 %collective-permute-start.20 = (f32[128,256]{1,0:T(8,128)S(1)}, f32[128,256]{1,0:T(8,128)S(1)}, u32[]{:S(2)}, u32[]{:S(2)}) collective-permute-start(f32[128,256]{1,0:T(8,128)S(1)} %get-tuple-element.147), channel_id=1, source_target_pairs={{0,1},{1,2},{2,3},{3,0},{4,5},{5,6},{6,7},{7,4},{8,9},{9,10},{10,1... | collective-permute-start | bytes 393224 | tf_op jit(solution)/shard_map/ppermute | solution.py:33
  47.6 0.8 %collective-permute-start.26 = (f32[128,256]{1,0:T(8,128)S(1)}, f32[128,256]{1,0:T(8,128)S(1)}, u32[]{:S(2)}, u32[]{:S(2)}) collective-permute-start(f32[128,256]{1,0:T(8,128)S(1)} %get-tuple-element.158), channel_id=1, source_target_pairs={{0,1},{1,2},{2,3},{3,0},{4,5},{5,6},{6,7},{7,4},{8,9},{9,10},{10,1... | collective-permute-start | bytes 393224 | tf_op jit(solution)/shard_map/ppermute | solution.py:33
  49.5 0.7 %collective-permute-done.20.piece_ref = f32[128,256]{1,0:T(8,128)S(1)} collective-permute-done((f32[128,256]{1,0:T(8,128)S(1)}, f32[128,256]{1,0:T(8,128)S(1)}, u32[]{:S(2)}, u32[]{:S(2)}) %collective-permute-start.20) | collective-permute-done | bytes 131104 | tf_op jit(solution)/shard_map/ppermute | solution.py:33
  50.8 0.8 %collective-permute-start.24 = (f32[128,256]{1,0:T(8,128)S(1)}, f32[128,256]{1,0:T(8,128)S(1)}, u32[]{:S(2)}, u32[]{:S(2)}) collective-permute-start(f32[128,256]{1,0:T(8,128)S(1)} %get-tuple-element.156), channel_id=1, source_target_pairs={{0,1},{1,2},{2,3},{3,0},{4,5},{5,6},{6,7},{7,4},{8,9},{9,10},{10,1... | collective-permute-start | bytes 393224 | tf_op jit(solution)/shard_map/ppermute | solution.py:33
  52.2 0.7 %collective-permute-start.27 = (f32[128,256]{1,0:T(8,128)S(1)}, f32[128,256]{1,0:T(8,128)S(1)}, u32[]{:S(2)}, u32[]{:S(2)}) collective-permute-start(f32[128,256]{1,0:T(8,128)S(1)} %get-tuple-element.162), channel_id=1, source_target_pairs={{0,1},{1,2},{2,3},{3,0},{4,5},{5,6},{6,7},{7,4},{8,9},{9,10},{10,1... | collective-permute-start | bytes 393224 | tf_op jit(solution)/shard_map/ppermute | solution.py:33
  53.4 0.9 %collective-permute-done.25.piece_ref = f32[128,256]{1,0:T(8,128)S(1)} collective-permute-done((f32[128,256]{1,0:T(8,128)S(1)}, f32[128,256]{1,0:T(8,128)S(1)}, u32[]{:S(2)}, u32[]{:S(2)}) %collective-permute-start.25) | collective-permute-done | bytes 131104 | tf_op jit(solution)/shard_map/ppermute | solution.py:33
  55.0 0.7 %collective-permute-done.24.piece_ref = f32[128,256]{1,0:T(8,128)S(1)} collective-permute-done((f32[128,256]{1,0:T(8,128)S(1)}, f32[128,256]{1,0:T(8,128)S(1)}, u32[]{:S(2)}, u32[]{:S(2)}) %collective-permute-start.24) | collective-permute-done | bytes 131104 | tf_op jit(solution)/shard_map/ppermute | solution.py:33
  56.4 0.8 %collective-permute-done.27.piece_ref = f32[128,256]{1,0:T(8,128)S(1)} collective-permute-done((f32[128,256]{1,0:T(8,128)S(1)}, f32[128,256]{1,0:T(8,128)S(1)}, u32[]{:S(2)}, u32[]{:S(2)}) %collective-permute-start.27) | collective-permute-done | bytes 131104 | tf_op jit(solution)/shard_map/ppermute | solution.py:33
  57.2 1.5 %shard_map.111 = (f32[512,256]{1,0:T(8,128)}, f32[512,256]{1,0:T(8,128)}) custom-call(f32[512,256]{1,0:T(8,128)S(1)} %get-tuple-element.154.user_ref, bf16[512,256]{1,0:T(8,128)(2,1)S(1)} %get-tuple-element.155.half_ref, f32[512,256]{1,0:T(8,128)S(1)} %get-tuple-element.161.grad_ref, f32[128,256]{1,0:T(8,128)S(1)} %collective-permute-done.27.piece_ref, ...), custom_call_target="tpu_custom_call" | custom-call | flops 100663296 | bytes 1024 | tf_op jit(solution)/shard_map/pallas_call | solution.py:286
  (63 shorter events, 18.4 us)
Async XLA Ops:
  4.2 5.3 %collective-permute-start.2 = (f32[128,256]{1,0:T(8,128)S(1)}, f32[128,256]{1,0:T(8,128)S(1)}, u32[]{:S(2)}, u32[]{:S(2)}) collective-permute-start(f32[128,256]{1,0:T(8,128)S(1)} %get-tuple-element.99), channel_id=1, source_target_pairs={{0,1},{1,2},{2,3},{3,0},{4,5},{5,6},{6,7},{7,4},{8,9},{9,10},{10,1... | collective-permute-start | bytes 393224 | tf_op jit(solution)/shard_map/ppermute | solution.py:33
  5.4 5.3 %collective-permute-start.1 = (f32[128,256]{1,0:T(8,128)S(1)}, f32[128,256]{1,0:T(8,128)S(1)}, u32[]{:S(2)}, u32[]{:S(2)}) collective-permute-start(f32[128,256]{1,0:T(8,128)S(1)} %get-tuple-element.98), channel_id=1, source_target_pairs={{0,1},{1,2},{2,3},{3,0},{4,5},{5,6},{6,7},{7,4},{8,9},{9,10},{10,1... | collective-permute-start | bytes 393224 | tf_op jit(solution)/shard_map/ppermute | solution.py:33
  8.7 4.4 %collective-permute-start = (f32[128,256]{1,0:T(8,128)S(1)}, f32[128,256]{1,0:T(8,128)S(1)}, u32[]{:S(2)}, u32[]{:S(2)}) collective-permute-start(f32[128,256]{1,0:T(8,128)S(1)} %get-tuple-element.97), channel_id=1, source_target_pairs={{0,1},{1,2},{2,3},{3,0},{4,5},{5,6},{6,7},{7,4},{8,9},{9,10},{10,1... | collective-permute-start | bytes 393224 | tf_op jit(solution)/shard_map/ppermute | solution.py:33
  9.4 5.2 %collective-permute-start.3 = (f32[128,256]{1,0:T(8,128)S(1)}, f32[128,256]{1,0:T(8,128)S(1)}, u32[]{:S(2)}, u32[]{:S(2)}) collective-permute-start(f32[128,256]{1,0:T(8,128)S(1)} %get-tuple-element.103), channel_id=1, source_target_pairs={{0,1},{1,2},{2,3},{3,0},{4,5},{5,6},{6,7},{7,4},{8,9},{9,10},{10,1... | collective-permute-start | bytes 393224 | tf_op jit(solution)/shard_map/ppermute | solution.py:33
  9.9 7.5 %collective-permute-start.6 = (f32[128,256]{1,0:T(8,128)S(1)}, f32[128,256]{1,0:T(8,128)S(1)}, u32[]{:S(2)}, u32[]{:S(2)}) collective-permute-start(f32[128,256]{1,0:T(8,128)S(1)} %get-tuple-element.111), channel_id=1, source_target_pairs={{0,1},{1,2},{2,3},{3,0},{4,5},{5,6},{6,7},{7,4},{8,9},{9,10},{10,1... | collective-permute-start | bytes 393224 | tf_op jit(solution)/shard_map/ppermute | solution.py:33
  10.7 5.2 %copy-start.1 = (bf16[512,8,512]{2,1,0:T(8,128)(2,1)S(1)}, bf16[512,8,512]{2,1,0:T(8,128)(2,1)}, u32[]{:S(2)}) copy-start(bf16[512,8,512]{2,1,0:T(8,128)(2,1)} %param.9) | copy-start | bytes 12582916
  11.4 7.2 %collective-permute-start.5 = (f32[128,256]{1,0:T(8,128)S(1)}, f32[128,256]{1,0:T(8,128)S(1)}, u32[]{:S(2)}, u32[]{:S(2)}) collective-permute-start(f32[128,256]{1,0:T(8,128)S(1)} %get-tuple-element.110), channel_id=1, source_target_pairs={{0,1},{1,2},{2,3},{3,0},{4,5},{5,6},{6,7},{7,4},{8,9},{9,10},{10,1... | collective-permute-start | bytes 393224 | tf_op jit(solution)/shard_map/ppermute | solution.py:33
  13.1 2.8 %copy-start = (bf16[512,8,512]{2,1,0:T(8,128)(2,1)S(1)}, bf16[512,8,512]{2,1,0:T(8,128)(2,1)}, u32[]{:S(2)}) copy-start(bf16[512,8,512]{2,1,0:T(8,128)(2,1)} %param.8) | copy-start | bytes 12582916
  13.8 5.9 %collective-permute-start.4 = (f32[128,256]{1,0:T(8,128)S(1)}, f32[128,256]{1,0:T(8,128)S(1)}, u32[]{:S(2)}, u32[]{:S(2)}) collective-permute-start(f32[128,256]{1,0:T(8,128)S(1)} %get-tuple-element.106), channel_id=1, source_target_pairs={{0,1},{1,2},{2,3},{3,0},{4,5},{5,6},{6,7},{7,4},{8,9},{9,10},{10,1... | collective-permute-start | bytes 393224 | tf_op jit(solution)/shard_map/ppermute | solution.py:33
  15.2 5.7 %collective-permute-start.7 = (f32[128,256]{1,0:T(8,128)S(1)}, f32[128,256]{1,0:T(8,128)S(1)}, u32[]{:S(2)}, u32[]{:S(2)}) collective-permute-start(f32[128,256]{1,0:T(8,128)S(1)} %get-tuple-element.115), channel_id=1, source_target_pairs={{0,1},{1,2},{2,3},{3,0},{4,5},{5,6},{6,7},{7,4},{8,9},{9,10},{10,1... | collective-permute-start | bytes 393224 | tf_op jit(solution)/shard_map/ppermute | solution.py:33
  17.9 4.4 %collective-permute-start.10 = (f32[128,256]{1,0:T(8,128)S(1)}, f32[128,256]{1,0:T(8,128)S(1)}, u32[]{:S(2)}, u32[]{:S(2)}) collective-permute-start(f32[128,256]{1,0:T(8,128)S(1)} %get-tuple-element.120), channel_id=1, source_target_pairs={{0,1},{1,2},{2,3},{3,0},{4,5},{5,6},{6,7},{7,4},{8,9},{9,10},{10,1... | collective-permute-start | bytes 393224 | tf_op jit(solution)/shard_map/ppermute | solution.py:33
  19.3 5.0 %collective-permute-start.9 = (f32[128,256]{1,0:T(8,128)S(1)}, f32[128,256]{1,0:T(8,128)S(1)}, u32[]{:S(2)}, u32[]{:S(2)}) collective-permute-start(f32[128,256]{1,0:T(8,128)S(1)} %get-tuple-element.119), channel_id=1, source_target_pairs={{0,1},{1,2},{2,3},{3,0},{4,5},{5,6},{6,7},{7,4},{8,9},{9,10},{10,1... | collective-permute-start | bytes 393224 | tf_op jit(solution)/shard_map/ppermute | solution.py:33
  20.3 6.3 %collective-permute-start.8 = (f32[128,256]{1,0:T(8,128)S(1)}, f32[128,256]{1,0:T(8,128)S(1)}, u32[]{:S(2)}, u32[]{:S(2)}) collective-permute-start(f32[128,256]{1,0:T(8,128)S(1)} %get-tuple-element.118), channel_id=1, source_target_pairs={{0,1},{1,2},{2,3},{3,0},{4,5},{5,6},{6,7},{7,4},{8,9},{9,10},{10,1... | collective-permute-start | bytes 393224 | tf_op jit(solution)/shard_map/ppermute | solution.py:33
  21.5 7.2 %collective-permute-start.11 = (f32[128,256]{1,0:T(8,128)S(1)}, f32[128,256]{1,0:T(8,128)S(1)}, u32[]{:S(2)}, u32[]{:S(2)}) collective-permute-start(f32[128,256]{1,0:T(8,128)S(1)} %get-tuple-element.124), channel_id=1, source_target_pairs={{0,1},{1,2},{2,3},{3,0},{4,5},{5,6},{6,7},{7,4},{8,9},{9,10},{10,1... | collective-permute-start | bytes 393224 | tf_op jit(solution)/shard_map/ppermute | solution.py:33
  22.8 9.1 %collective-permute-start.14 = (f32[128,256]{1,0:T(8,128)S(1)}, f32[128,256]{1,0:T(8,128)S(1)}, u32[]{:S(2)}, u32[]{:S(2)}) collective-permute-start(f32[128,256]{1,0:T(8,128)S(1)} %get-tuple-element.129), channel_id=1, source_target_pairs={{0,4},{4,8},{8,12},{12,16},{16,20},{20,24},{24,28},{28,0},{1,5},{5... | collective-permute-start | bytes 393224 | tf_op jit(solution)/shard_map/ppermute | solution.py:33
  25.0 9.7 %collective-permute-start.13 = (f32[128,256]{1,0:T(8,128)S(1)}, f32[128,256]{1,0:T(8,128)S(1)}, u32[]{:S(2)}, u32[]{:S(2)}) collective-permute-start(f32[128,256]{1,0:T(8,128)S(1)} %get-tuple-element.128), channel_id=1, source_target_pairs={{0,4},{4,8},{8,12},{12,16},{16,20},{20,24},{24,28},{28,0},{1,5},{5... | collective-permute-start | bytes 393224 | tf_op jit(solution)/shard_map/ppermute | solution.py:33
  27.2 10.3 %collective-permute-start.12 = (f32[128,256]{1,0:T(8,128)S(1)}, f32[128,256]{1,0:T(8,128)S(1)}, u32[]{:S(2)}, u32[]{:S(2)}) collective-permute-start(f32[128,256]{1,0:T(8,128)S(1)} %get-tuple-element.127), channel_id=1, source_target_pairs={{0,4},{4,8},{8,12},{12,16},{16,20},{20,24},{24,28},{28,0},{1,5},{5... | collective-permute-start | bytes 393224 | tf_op jit(solution)/shard_map/ppermute | solution.py:33
  29.4 10.7 %collective-permute-start.15 = (f32[128,256]{1,0:T(8,128)S(1)}, f32[128,256]{1,0:T(8,128)S(1)}, u32[]{:S(2)}, u32[]{:S(2)}) collective-permute-start(f32[128,256]{1,0:T(8,128)S(1)} %get-tuple-element.133), channel_id=1, source_target_pairs={{0,4},{4,8},{8,12},{12,16},{16,20},{20,24},{24,28},{28,0},{1,5},{5... | collective-permute-start | bytes 393224 | tf_op jit(solution)/shard_map/ppermute | solution.py:33
  32.4 9.9 %collective-permute-start.18 = (f32[128,256]{1,0:T(8,128)S(1)}, f32[128,256]{1,0:T(8,128)S(1)}, u32[]{:S(2)}, u32[]{:S(2)}) collective-permute-start(f32[128,256]{1,0:T(8,128)S(1)} %get-tuple-element.140), channel_id=1, source_target_pairs={{0,1},{1,2},{2,3},{3,0},{4,5},{5,6},{6,7},{7,4},{8,9},{9,10},{10,1... | collective-permute-start | bytes 393224 | tf_op jit(solution)/shard_map/ppermute | solution.py:33
  35.4 8.3 %collective-permute-start.17 = (f32[128,256]{1,0:T(8,128)S(1)}, f32[128,256]{1,0:T(8,128)S(1)}, u32[]{:S(2)}, u32[]{:S(2)}) collective-permute-start(f32[128,256]{1,0:T(8,128)S(1)} %get-tuple-element.139), channel_id=1, source_target_pairs={{0,1},{1,2},{2,3},{3,0},{4,5},{5,6},{6,7},{7,4},{8,9},{9,10},{10,1... | collective-permute-start | bytes 393224 | tf_op jit(solution)/shard_map/ppermute | solution.py:33
  38.1 6.2 %collective-permute-start.16 = (f32[128,256]{1,0:T(8,128)S(1)}, f32[128,256]{1,0:T(8,128)S(1)}, u32[]{:S(2)}, u32[]{:S(2)}) collective-permute-start(f32[128,256]{1,0:T(8,128)S(1)} %get-tuple-element.136), channel_id=1, source_target_pairs={{0,1},{1,2},{2,3},{3,0},{4,5},{5,6},{6,7},{7,4},{8,9},{9,10},{10,1... | collective-permute-start | bytes 393224 | tf_op jit(solution)/shard_map/ppermute | solution.py:33
  40.7 5.7 %collective-permute-start.19 = (f32[128,256]{1,0:T(8,128)S(1)}, f32[128,256]{1,0:T(8,128)S(1)}, u32[]{:S(2)}, u32[]{:S(2)}) collective-permute-start(f32[128,256]{1,0:T(8,128)S(1)} %get-tuple-element.144), channel_id=1, source_target_pairs={{0,1},{1,2},{2,3},{3,0},{4,5},{5,6},{6,7},{7,4},{8,9},{9,10},{10,1... | collective-permute-start | bytes 393224 | tf_op jit(solution)/shard_map/ppermute | solution.py:33
  42.7 4.4 %collective-permute-start.22 = (f32[128,256]{1,0:T(8,128)S(1)}, f32[128,256]{1,0:T(8,128)S(1)}, u32[]{:S(2)}, u32[]{:S(2)}) collective-permute-start(f32[128,256]{1,0:T(8,128)S(1)} %get-tuple-element.149), channel_id=1, source_target_pairs={{0,1},{1,2},{2,3},{3,0},{4,5},{5,6},{6,7},{7,4},{8,9},{9,10},{10,1... | collective-permute-start | bytes 393224 | tf_op jit(solution)/shard_map/ppermute | solution.py:33
  44.3 4.4 %collective-permute-start.21 = (f32[128,256]{1,0:T(8,128)S(1)}, f32[128,256]{1,0:T(8,128)S(1)}, u32[]{:S(2)}, u32[]{:S(2)}) collective-permute-start(f32[128,256]{1,0:T(8,128)S(1)} %get-tuple-element.148), channel_id=1, source_target_pairs={{0,1},{1,2},{2,3},{3,0},{4,5},{5,6},{6,7},{7,4},{8,9},{9,10},{10,1... | collective-permute-start | bytes 393224 | tf_op jit(solution)/shard_map/ppermute | solution.py:33
  45.0 5.2 %collective-permute-start.20 = (f32[128,256]{1,0:T(8,128)S(1)}, f32[128,256]{1,0:T(8,128)S(1)}, u32[]{:S(2)}, u32[]{:S(2)}) collective-permute-start(f32[128,256]{1,0:T(8,128)S(1)} %get-tuple-element.147), channel_id=1, source_target_pairs={{0,1},{1,2},{2,3},{3,0},{4,5},{5,6},{6,7},{7,4},{8,9},{9,10},{10,1... | collective-permute-start | bytes 393224 | tf_op jit(solution)/shard_map/ppermute | solution.py:33
  47.1 4.5 %collective-permute-start.23 = (f32[128,256]{1,0:T(8,128)S(1)}, f32[128,256]{1,0:T(8,128)S(1)}, u32[]{:S(2)}, u32[]{:S(2)}) collective-permute-start(f32[128,256]{1,0:T(8,128)S(1)} %get-tuple-element.153), channel_id=1, source_target_pairs={{0,1},{1,2},{2,3},{3,0},{4,5},{5,6},{6,7},{7,4},{8,9},{9,10},{10,1... | collective-permute-start | bytes 393224 | tf_op jit(solution)/shard_map/ppermute | solution.py:33
  47.6 5.3 %collective-permute-start.26 = (f32[128,256]{1,0:T(8,128)S(1)}, f32[128,256]{1,0:T(8,128)S(1)}, u32[]{:S(2)}, u32[]{:S(2)}) collective-permute-start(f32[128,256]{1,0:T(8,128)S(1)} %get-tuple-element.158), channel_id=1, source_target_pairs={{0,1},{1,2},{2,3},{3,0},{4,5},{5,6},{6,7},{7,4},{8,9},{9,10},{10,1... | collective-permute-start | bytes 393224 | tf_op jit(solution)/shard_map/ppermute | solution.py:33
  49.4 5.0 %collective-permute-start.25 = (f32[128,256]{1,0:T(8,128)S(1)}, f32[128,256]{1,0:T(8,128)S(1)}, u32[]{:S(2)}, u32[]{:S(2)}) collective-permute-start(f32[128,256]{1,0:T(8,128)S(1)} %get-tuple-element.157), channel_id=1, source_target_pairs={{0,1},{1,2},{2,3},{3,0},{4,5},{5,6},{6,7},{7,4},{8,9},{9,10},{10,1... | collective-permute-start | bytes 393224 | tf_op jit(solution)/shard_map/ppermute | solution.py:33
  50.8 5.0 %collective-permute-start.24 = (f32[128,256]{1,0:T(8,128)S(1)}, f32[128,256]{1,0:T(8,128)S(1)}, u32[]{:S(2)}, u32[]{:S(2)}) collective-permute-start(f32[128,256]{1,0:T(8,128)S(1)} %get-tuple-element.156), channel_id=1, source_target_pairs={{0,1},{1,2},{2,3},{3,0},{4,5},{5,6},{6,7},{7,4},{8,9},{9,10},{10,1... | collective-permute-start | bytes 393224 | tf_op jit(solution)/shard_map/ppermute | solution.py:33
  52.2 5.0 %collective-permute-start.27 = (f32[128,256]{1,0:T(8,128)S(1)}, f32[128,256]{1,0:T(8,128)S(1)}, u32[]{:S(2)}, u32[]{:S(2)}) collective-permute-start(f32[128,256]{1,0:T(8,128)S(1)} %get-tuple-element.162), channel_id=1, source_target_pairs={{0,1},{1,2},{2,3},{3,0},{4,5},{5,6},{6,7},{7,4},{8,9},{9,10},{10,1... | collective-permute-start | bytes 393224 | tf_op jit(solution)/shard_map/ppermute | solution.py:33
where the time goes:
time: 59 us; the launch traced here: 58.8 us
  Pallas kernels  25.7 us (44%)
  starting transfers between devices  20.6 us (35%)
  waiting for transfers between devices  11.5 us (19%)
  between operations  1.1 us (2%)
    ppermute x28, starting transfers between devices, from_behind(): return lax.ppermute(value, axis, pairs)  20.6 us
    ppermute x28, waiting for transfers between devices, from_behind(): return lax.ppermute(value, axis, pairs)  11.5 us
    pallas_call x16, Pallas kernels, middle_piece(): call(kernel, (jax.ShapeDtypeStruct((m, rank), f32), jax.ShapeDtypeStruct(...  10.2 us
    pallas_call x7, Pallas kernels, last_piece(): call(kernel, (jax.ShapeDtypeStruct((m, rank), f32), jax.ShapeDtypeStruct(...  4.32 us
    pallas_call x8, Pallas kernels, first_piece(): call(kernel, (jax.ShapeDtypeStruct((m, rank), f32), jax.ShapeDtypeStruct(...  3.66 us
    pallas_call x1, Pallas kernels, load(): call(kernel, (table, table, jax.ShapeDtypeStruct((strata, items), f32), j...  3.09 us
    pallas_call x2, Pallas kernels, sort_strata(): call(kernel, (table, table), [VMEM] * 3, (VMEM, VMEM), 4 * kept * users *...  2.92 us
    pallas_call x1, Pallas kernels, finish(): call(kernel, (jax.ShapeDtypeStruct((users, rank), f32), jax.ShapeDtypeStr...  1.49 us
  transfers between devices with their start and end apart: 28, of which 12 were waited for; matrix products, arithmetic and copies ran while one was open for 0% of the time, Pallas kernels for 35%

commit v1 on v0

--- a/solution.py
+++ b/solution.py
@@ -211,6 +211,29 @@
     )(user_half, piece, ratings, weights)
 
 
+def users_step(user_rows, residuals, pieces):
+    count = len(pieces)
+
+    def kernel(user_ref, *refs):
+        residual_refs, piece_refs, (user_out, half_out) = refs[:count], refs[count : 2 * count], refs[2 * count :]
+        user = user_ref[...]
+        grad = ridge_weight * user
+        for residual_ref, piece_ref in zip(residual_refs, piece_refs):
+            grad += users_grad(residual_ref[...], piece_ref[...])
+        user = user - learn_rate * grad
+        user_out[...] = user
+        half_out[...] = user.astype(bf16)
+
+    users, rank = user_rows.shape
+    return call(
+        kernel,
+        (jax.ShapeDtypeStruct((users, rank), f32), jax.ShapeDtypeStruct((users, rank), bf16)),
+        [VMEM] * (1 + 2 * count),
+        (VMEM, VMEM),
+        2 * users * rank * users,
+    )(user_rows, *residuals, *pieces)
+
+
 def middle_piece(stratum, cols, user_rows, user_half, piece, ratings, weights, earlier):
     def kernel(user_ref, half_ref, piece_ref, rating_ref, weight_ref, *refs):
         earlier_refs, (new_ref, grad_ref) = refs[:-2], refs[-2:]
@@ -231,29 +254,6 @@
         (VMEM, VMEM),
         8 * users * m * rank,
     )(user_rows, user_half, piece, ratings, weights, *earlier)
-
-
-def last_piece(stratum, cols, user_rows, user_half, grad, piece, ratings, weights):
-    def kernel(user_ref, half_ref, grad_ref, piece_ref, rating_ref, weight_ref, new_ref, user_out, half_out):
-        rows = piece_ref[...]
-        residual, new_ref[...] = piece_step(half_ref[...], rows, rating_ref, weight_ref, stratum, cols)
-        user = user_ref[...] - learn_rate * (grad_ref[...] + users_grad(residual, rows))
-        user_out[...] = user
-        half_out[...] = user.astype(bf16)
-
-    users = user_half.shape[0]
-    m, rank = piece.shape
-    return call(
-        kernel,
-        (
-            jax.ShapeDtypeStruct((m, rank), f32),
-            jax.ShapeDtypeStruct((users, rank), f32),
-            jax.ShapeDtypeStruct((users, rank), bf16),
-        ),
-        [VMEM] * 6,
-        (VMEM,) * 3,
-        6 * users * m * rank,
-    )(user_rows, user_half, grad, piece, ratings, weights)
 
 
 def finish(stratum, cols, user_rows, user_half, grad, piece, ratings, weights, news):
@@ -316,21 +316,22 @@
             def move(new):
                 return move_items(new, outer_step, inner_step)
 
-            new, residual = first_piece(row, cols[0], user_half, pieces[0], rating, weight)
-            news = [move(new)]
-            earlier = (pieces[0], residual)
-            for j in range(1, last):
-                new, grad = middle_piece(row, cols[j], user_rows, user_half, pieces[j], rating, weight, earlier)
+            final = stratum == S_OUT * S_IN - 1
+            news, residuals = [], []
+            if final:
+                new, residual = first_piece(row, cols[0], user_half, pieces[0], rating, weight)
+                news = [new]
+                earlier = (pieces[0], residual)
+                for j in range(1, last):
+                    new, grad = middle_piece(row, cols[j], user_rows, user_half, pieces[j], rating, weight, earlier)
+                    news.append(new)
+                    earlier = (grad,)
+                return finish(row, cols[last], user_rows, user_half, grad, pieces[last], rating, weight, news)
+            for j in range(last + 1):
+                new, residual = first_piece(row, cols[j], user_half, pieces[j], rating, weight)
+                residuals.append(residual)
                 news.append(move(new))
-                earlier = (grad,)
-            if stratum == S_OUT * S_IN - 1:
-                return finish(
-                    row, cols[last], user_rows, user_half, grad, pieces[last], rating, weight, news
-                )
-            new, user_rows, user_half = last_piece(
-                row, cols[last], user_rows, user_half, grad, pieces[last], rating, weight
-            )
-            news.append(move(new))
+            user_rows, user_half = users_step(user_rows, residuals, pieces)
             pieces = news
 
 

time: 59 us -> 59.5 us (level)
  waiting for transfers between devices: 11.5 us -> 13 us
  Pallas kernels: 25.7 us -> 25 us
    pallas_call x8 -> x29, Pallas kernels: 3.66 us -> 13.2 us  [first_piece(): call(kernel, (jax.ShapeDtypeStruct((m, rank), f32), jax.ShapeDtypeStruct(...]
    pallas_call x16 -> x2, Pallas kernels: 10.2 us -> 1.27 us  [middle_piece(): call(kernel, (jax.ShapeDtypeStruct((m, rank), f32), jax.ShapeDtypeStruct(...]
    ppermute x28, waiting for transfers between devices: 11.5 us -> 13 us  [from_behind(): return lax.ppermute(value, axis, pairs)]
    pallas_call x7, Pallas kernels: 4.32 us -> 2.97 us  [users_step(): call(kernel, (jax.ShapeDtypeStruct((users, rank), f32), jax.ShapeDtypeStr...]
  transfers between devices with their start and end apart: 28 -> 28, of which waited for: 12 -> 13; matrix products, arithmetic and copies ran while one was open for 0% -> 0% of each run, Pallas kernels for 35% -> 34%
where the time goes in v1:
time: 59.5 us; the launch traced here: 59.3 us
  Pallas kernels  25 us (42%)
  starting transfers between devices  20.1 us (34%)
  waiting for transfers between devices  13 us (22%)
  between operations  1.2 us (2%)
    ppermute x28, starting transfers between devices, from_behind(): return lax.ppermute(value, axis, pairs)  20.1 us
    pallas_call x29, Pallas kernels, first_piece(): call(kernel, (jax.ShapeDtypeStruct((m, rank), f32), jax.ShapeDtypeStruct(...  13.2 us
    ppermute x28, waiting for transfers between devices, from_behind(): return lax.ppermute(value, axis, pairs)  13 us
    pallas_call x1, Pallas kernels, load(): call(kernel, (table, table, jax.ShapeDtypeStruct((strata, items), f32), j...  3.09 us
    pallas_call x7, Pallas kernels, users_step(): call(kernel, (jax.ShapeDtypeStruct((users, rank), f32), jax.ShapeDtypeStr...  2.97 us
    pallas_call x2, Pallas kernels, sort_strata(): call(kernel, (table, table), [VMEM] * 3, (VMEM, VMEM), 4 * kept * users *...  2.92 us
    pallas_call x1, Pallas kernels, finish(): call(kernel, (jax.ShapeDtypeStruct((users, rank), f32), jax.ShapeDtypeStr...  1.49 us
    pallas_call x2, Pallas kernels, middle_piece(): call(kernel, (jax.ShapeDtypeStruct((m, rank), f32), jax.ShapeDtypeStruct(...  1.27 us
  transfers between devices with their start and end apart: 28, of which 13 were waited for; matrix products, arithmetic and copies ran while one was open for 0% of the time, Pallas kernels for 34%

profile of v1, /device:TPU:0, one launch (start us, length us, event | category | flops | bytes accessed | tf_op | source)
XLA Modules:
  0.0 59.3 jit_solution(12779763843588976498)
XLA Ops:
  0.6 3.1 %shard_map.77 = (bf16[2,512,512]{2,1,0:T(8,128)(2,1)S(1)}, bf16[2,512,512]{2,1,0:T(8,128)(2,1)S(1)}, f32[8,512]{1,0:T(8,128)S(1)}, f32[512,256]{1,0:T(8,128)S(1)...) custom-call(s32[4,8]{1,0:T(4,128)} %bitcast.21, ...), custom_call_target="tpu_custom_call" | custom-call | flops 268435456 | bytes 1024 | tf_op jit(solution)/shard_map/pallas_call | solution.py:131
  3.7 0.5 shard_map.78
  4.2 0.5 collective-permute-start
  5.2 2.7 %collective-permute-start.1 = (f32[128,256]{1,0:T(8,128)S(1)}, f32[128,256]{1,0:T(8,128)S(1)}, u32[]{:S(2)}, u32[]{:S(2)}) collective-permute-start(f32[128,256]{1,0:T(8,128)S(1)} %get-tuple-element.107), channel_id=1, source_target_pairs={{0,1},{1,2},{2,3},{3,0},{4,5},{5,6},{6,7},{7,4},{8,9},{9,10},{10,1... | collective-permute-start | bytes 393224 | tf_op jit(solution)/shard_map/ppermute | solution.py:33
  9.9 0.8 %collective-permute-done.1.piece_ref.refs_5_ = f32[128,256]{1,0:T(8,128)S(1)} collective-permute-done((f32[128,256]{1,0:T(8,128)S(1)}, f32[128,256]{1,0:T(8,128)S(1)}, u32[]{:S(2)}, u32[]{:S(2)}) %collective-permute-start.1) | collective-permute-done | bytes 131104 | tf_op jit(solution)/shard_map/ppermute | solution.py:33
  11.2 1.6 %collective-permute-start.5 = (f32[128,256]{1,0:T(8,128)S(1)}, f32[128,256]{1,0:T(8,128)S(1)}, u32[]{:S(2)}, u32[]{:S(2)}) collective-permute-start(f32[128,256]{1,0:T(8,128)S(1)} %get-tuple-element.120), channel_id=1, source_target_pairs={{0,1},{1,2},{2,3},{3,0},{4,5},{5,6},{6,7},{7,4},{8,9},{9,10},{10,1... | collective-permute-start | bytes 393224 | tf_op jit(solution)/shard_map/ppermute | solution.py:33
  13.3 0.9 %collective-permute-start.6 = (f32[128,256]{1,0:T(8,128)S(1)}, f32[128,256]{1,0:T(8,128)S(1)}, u32[]{:S(2)}, u32[]{:S(2)}) collective-permute-start(f32[128,256]{1,0:T(8,128)S(1)} %get-tuple-element.122), channel_id=1, source_target_pairs={{0,1},{1,2},{2,3},{3,0},{4,5},{5,6},{6,7},{7,4},{8,9},{9,10},{10,1... | collective-permute-start | bytes 393224 | tf_op jit(solution)/shard_map/ppermute | solution.py:33
  14.7 0.9 %collective-permute-start.7 = (f32[128,256]{1,0:T(8,128)S(1)}, f32[128,256]{1,0:T(8,128)S(1)}, u32[]{:S(2)}, u32[]{:S(2)}) collective-permute-start(f32[128,256]{1,0:T(8,128)S(1)} %get-tuple-element.124), channel_id=1, source_target_pairs={{0,1},{1,2},{2,3},{3,0},{4,5},{5,6},{6,7},{7,4},{8,9},{9,10},{10,1... | collective-permute-start | bytes 393224 | tf_op jit(solution)/shard_map/ppermute | solution.py:33
  15.6 1.5 %shard_map.88 = (bf16[3,512,512]{2,1,0:T(8,128)(2,1)S(1)}, bf16[3,512,512]{2,1,0:T(8,128)(2,1)S(1)}) custom-call(bf16[4096,512]{1,0:T(8,128)(2,1)S(1)} %bitcast.16, bf16[4096,512]{1,0:T(8,128)(2,1)S(1)} %bitcast.19, f32[8,512]{1,0:T(8,128)S(1)} %get-tuple-element.116.mask_ref), custom_call_target="tpu_custom_call" | custom-call | flops 805306368 | bytes 1024 | tf_op jit(solution)/shard_map/pallas_call | solution.py:179
  18.0 0.9 %collective-permute-start.8 = (f32[128,256]{1,0:T(8,128)S(1)}, f32[128,256]{1,0:T(8,128)S(1)}, u32[]{:S(2)}, u32[]{:S(2)}) collective-permute-start(f32[128,256]{1,0:T(8,128)S(1)} %get-tuple-element.128), channel_id=1, source_target_pairs={{0,1},{1,2},{2,3},{3,0},{4,5},{5,6},{6,7},{7,4},{8,9},{9,10},{10,1... | collective-permute-start | bytes 393224 | tf_op jit(solution)/shard_map/ppermute | solution.py:33
  20.9 0.9 %collective-permute-start.11 = (f32[128,256]{1,0:T(8,128)S(1)}, f32[128,256]{1,0:T(8,128)S(1)}, u32[]{:S(2)}, u32[]{:S(2)}) collective-permute-start(f32[128,256]{1,0:T(8,128)S(1)} %get-tuple-element.134), channel_id=1, source_target_pairs={{0,1},{1,2},{2,3},{3,0},{4,5},{5,6},{6,7},{7,4},{8,9},{9,10},{10,1... | collective-permute-start | bytes 393224 | tf_op jit(solution)/shard_map/ppermute | solution.py:33
  22.9 1.5 %collective-permute-start.12 = (f32[128,256]{1,0:T(8,128)S(1)}, f32[128,256]{1,0:T(8,128)S(1)}, u32[]{:S(2)}, u32[]{:S(2)}) collective-permute-start(f32[128,256]{1,0:T(8,128)S(1)} %get-tuple-element.138), channel_id=1, source_target_pairs={{0,4},{4,8},{8,12},{12,16},{16,20},{20,24},{24,28},{28,0},{1,5},{5... | collective-permute-start | bytes 393224 | tf_op jit(solution)/shard_map/ppermute | solution.py:33
  24.9 1.6 %collective-permute-start.13 = (f32[128,256]{1,0:T(8,128)S(1)}, f32[128,256]{1,0:T(8,128)S(1)}, u32[]{:S(2)}, u32[]{:S(2)}) collective-permute-start(f32[128,256]{1,0:T(8,128)S(1)} %get-tuple-element.140), channel_id=1, source_target_pairs={{0,4},{4,8},{8,12},{12,16},{16,20},{20,24},{24,28},{28,0},{1,5},{5... | collective-permute-start | bytes 393224 | tf_op jit(solution)/shard_map/ppermute | solution.py:33
  27.0 1.5 %collective-permute-start.14 = (f32[128,256]{1,0:T(8,128)S(1)}, f32[128,256]{1,0:T(8,128)S(1)}, u32[]{:S(2)}, u32[]{:S(2)}) collective-permute-start(f32[128,256]{1,0:T(8,128)S(1)} %get-tuple-element.142), channel_id=1, source_target_pairs={{0,4},{4,8},{8,12},{12,16},{16,20},{20,24},{24,28},{28,0},{1,5},{5... | collective-permute-start | bytes 393224 | tf_op jit(solution)/shard_map/ppermute | solution.py:33
  29.0 1.6 %collective-permute-start.15 = (f32[128,256]{1,0:T(8,128)S(1)}, f32[128,256]{1,0:T(8,128)S(1)}, u32[]{:S(2)}, u32[]{:S(2)}) collective-permute-start(f32[128,256]{1,0:T(8,128)S(1)} %get-tuple-element.144), channel_id=1, source_target_pairs={{0,4},{4,8},{8,12},{12,16},{16,20},{20,24},{24,28},{28,0},{1,5},{5... | collective-permute-start | bytes 393224 | tf_op jit(solution)/shard_map/ppermute | solution.py:33
  31.0 1.0 %collective-permute-done.12.piece_ref.refs_4_ = f32[128,256]{1,0:T(8,128)S(1)} collective-permute-done((f32[128,256]{1,0:T(8,128)S(1)}, f32[128,256]{1,0:T(8,128)S(1)}, u32[]{:S(2)}, u32[]{:S(2)}) %collective-permute-start.12) | collective-permute-done | bytes 131104 | tf_op jit(solution)/shard_map/ppermute | solution.py:33
  32.5 2.3 %collective-permute-done.13.piece_ref.refs_5_ = f32[128,256]{1,0:T(8,128)S(1)} collective-permute-done((f32[128,256]{1,0:T(8,128)S(1)}, f32[128,256]{1,0:T(8,128)S(1)}, u32[]{:S(2)}, u32[]{:S(2)}) %collective-permute-start.13) | collective-permute-done | bytes 131104 | tf_op jit(solution)/shard_map/ppermute | solution.py:33
  35.3 2.3 %collective-permute-done.14.piece_ref.refs_6_ = f32[128,256]{1,0:T(8,128)S(1)} collective-permute-done((f32[128,256]{1,0:T(8,128)S(1)}, f32[128,256]{1,0:T(8,128)S(1)}, u32[]{:S(2)}, u32[]{:S(2)}) %collective-permute-start.14) | collective-permute-done | bytes 131104 | tf_op jit(solution)/shard_map/ppermute | solution.py:33
  38.1 2.2 %collective-permute-done.15.piece_ref.refs_7_ = f32[128,256]{1,0:T(8,128)S(1)} collective-permute-done((f32[128,256]{1,0:T(8,128)S(1)}, f32[128,256]{1,0:T(8,128)S(1)}, u32[]{:S(2)}, u32[]{:S(2)}) %collective-permute-start.15) | collective-permute-done | bytes 131104 | tf_op jit(solution)/shard_map/ppermute | solution.py:33
  41.0 1.5 %shard_map.104 = (bf16[3,512,512]{2,1,0:T(8,128)(2,1)S(1)}, bf16[3,512,512]{2,1,0:T(8,128)(2,1)S(1)}) custom-call(bf16[4096,512]{1,0:T(8,128)(2,1)S(1)} %bitcast.17, bf16[4096,512]{1,0:T(8,128)(2,1)S(1)} %bitcast.20, f32[8,512]{1,0:T(8,128)S(1)} %get-tuple-element.116.mask_ref), custom_call_target="tpu_custom_call" | custom-call | flops 805306368 | bytes 1024 | tf_op jit(solution)/shard_map/pallas_call | solution.py:179
  43.4 0.7 %collective-permute-start.20 = (f32[128,256]{1,0:T(8,128)S(1)}, f32[128,256]{1,0:T(8,128)S(1)}, u32[]{:S(2)}, u32[]{:S(2)}) collective-permute-start(f32[128,256]{1,0:T(8,128)S(1)} %get-tuple-element.160), channel_id=1, source_target_pairs={{0,1},{1,2},{2,3},{3,0},{4,5},{5,6},{6,7},{7,4},{8,9},{9,10},{10,1... | collective-permute-start | bytes 393224 | tf_op jit(solution)/shard_map/ppermute | solution.py:33
  45.1 1.7 %collective-permute-start.22 = (f32[128,256]{1,0:T(8,128)S(1)}, f32[128,256]{1,0:T(8,128)S(1)}, u32[]{:S(2)}, u32[]{:S(2)}) collective-permute-start(f32[128,256]{1,0:T(8,128)S(1)} %get-tuple-element.164), channel_id=1, source_target_pairs={{0,1},{1,2},{2,3},{3,0},{4,5},{5,6},{6,7},{7,4},{8,9},{9,10},{10,1... | collective-permute-start | bytes 393224 | tf_op jit(solution)/shard_map/ppermute | solution.py:33
  48.3 0.5 collective-permute-start.26
  49.8 0.9 %collective-permute-done.22.piece_ref.refs_6_ = f32[128,256]{1,0:T(8,128)S(1)} collective-permute-done((f32[128,256]{1,0:T(8,128)S(1)}, f32[128,256]{1,0:T(8,128)S(1)}, u32[]{:S(2)}, u32[]{:S(2)}) %collective-permute-start.22) | collective-permute-done | bytes 131104 | tf_op jit(solution)/shard_map/ppermute | solution.py:33
  51.1 0.5 collective-permute-start.24
  52.5 0.5 collective-permute-start.27
  53.9 0.9 %collective-permute-done.25.piece_ref = f32[128,256]{1,0:T(8,128)S(1)} collective-permute-done((f32[128,256]{1,0:T(8,128)S(1)}, f32[128,256]{1,0:T(8,128)S(1)}, u32[]{:S(2)}, u32[]{:S(2)}) %collective-permute-start.25) | collective-permute-done | bytes 131104 | tf_op jit(solution)/shard_map/ppermute | solution.py:33
  54.9 0.7 %shard_map.116 = (f32[128,256]{1,0:T(8,128)S(1)}, f32[512,256]{1,0:T(8,128)S(1)}) custom-call(f32[512,256]{1,0:T(8,128)S(1)} %get-tuple-element.168.user_ref, bf16[512,256]{1,0:T(8,128)(2,1)S(1)} %get-tuple-element.169.half_ref, f32[128,256]{1,0:T(8,128)S(1)} %collective-permute-done.25.piece_ref, bf16[3,512,512]{2,1,0:T(8,128)(2,1)S(1)} %get-tuple-element.149.rating_ref, ...), custom_call_target="tpu_custom_call" | custom-call | flops 134217728 | bytes 1024 | tf_op jit(solution)/shard_map/pallas_call | solution.py:250
  55.5 0.7 %collective-permute-done.24.piece_ref = f32[128,256]{1,0:T(8,128)S(1)} collective-permute-done((f32[128,256]{1,0:T(8,128)S(1)}, f32[128,256]{1,0:T(8,128)S(1)}, u32[]{:S(2)}, u32[]{:S(2)}) %collective-permute-start.24) | collective-permute-done | bytes 131104 | tf_op jit(solution)/shard_map/ppermute | solution.py:33
  56.3 0.6 %shard_map.117 = (f32[128,256]{1,0:T(8,128)S(1)}, f32[512,256]{1,0:T(8,128)S(1)}) custom-call(f32[512,256]{1,0:T(8,128)S(1)} %get-tuple-element.168.user_ref, bf16[512,256]{1,0:T(8,128)(2,1)S(1)} %get-tuple-element.169.half_ref, f32[128,256]{1,0:T(8,128)S(1)} %collective-permute-done.24.piece_ref, bf16[3,512,512]{2,1,0:T(8,128)(2,1)S(1)} %get-tuple-element.149.rating_ref, ...), custom_call_target="tpu_custom_call" | custom-call | flops 134217728 | bytes 1024 | tf_op jit(solution)/shard_map/pallas_call | solution.py:250
  56.9 0.8 %collective-permute-done.27.piece_ref = f32[128,256]{1,0:T(8,128)S(1)} collective-permute-done((f32[128,256]{1,0:T(8,128)S(1)}, f32[128,256]{1,0:T(8,128)S(1)}, u32[]{:S(2)}, u32[]{:S(2)}) %collective-permute-start.27) | collective-permute-done | bytes 131104 | tf_op jit(solution)/shard_map/ppermute | solution.py:33
  57.7 1.5 %shard_map.118 = (f32[512,256]{1,0:T(8,128)}, f32[512,256]{1,0:T(8,128)}) custom-call(f32[512,256]{1,0:T(8,128)S(1)} %get-tuple-element.168.user_ref, bf16[512,256]{1,0:T(8,128)(2,1)S(1)} %get-tuple-element.169.half_ref, f32[512,256]{1,0:T(8,128)S(1)} %get-tuple-element.175.grad_ref, f32[128,256]{1,0:T(8,128)S(1)} %collective-permute-done.27.piece_ref, ...), custom_call_target="tpu_custom_call" | custom-call | flops 100663296 | bytes 1024 | tf_op jit(solution)/shard_map/pallas_call | solution.py:286
  (70 shorter events, 18.3 us)
Async XLA Ops:
  4.2 5.2 %collective-permute-start = (f32[128,256]{1,0:T(8,128)S(1)}, f32[128,256]{1,0:T(8,128)S(1)}, u32[]{:S(2)}, u32[]{:S(2)}) collective-permute-start(f32[128,256]{1,0:T(8,128)S(1)} %get-tuple-element.105), channel_id=1, source_target_pairs={{0,1},{1,2},{2,3},{3,0},{4,5},{5,6},{6,7},{7,4},{8,9},{9,10},{10,1... | collective-permute-start | bytes 393224 | tf_op jit(solution)/shard_map/ppermute | solution.py:33
  5.2 5.5 %collective-permute-start.1 = (f32[128,256]{1,0:T(8,128)S(1)}, f32[128,256]{1,0:T(8,128)S(1)}, u32[]{:S(2)}, u32[]{:S(2)}) collective-permute-start(f32[128,256]{1,0:T(8,128)S(1)} %get-tuple-element.107), channel_id=1, source_target_pairs={{0,1},{1,2},{2,3},{3,0},{4,5},{5,6},{6,7},{7,4},{8,9},{9,10},{10,1... | collective-permute-start | bytes 393224 | tf_op jit(solution)/shard_map/ppermute | solution.py:33
  8.3 4.5 %collective-permute-start.2 = (f32[128,256]{1,0:T(8,128)S(1)}, f32[128,256]{1,0:T(8,128)S(1)}, u32[]{:S(2)}, u32[]{:S(2)}) collective-permute-start(f32[128,256]{1,0:T(8,128)S(1)} %get-tuple-element.109), channel_id=1, source_target_pairs={{0,1},{1,2},{2,3},{3,0},{4,5},{5,6},{6,7},{7,4},{8,9},{9,10},{10,1... | collective-permute-start | bytes 393224 | tf_op jit(solution)/shard_map/ppermute | solution.py:33
  8.9 5.3 %collective-permute-start.3 = (f32[128,256]{1,0:T(8,128)S(1)}, f32[128,256]{1,0:T(8,128)S(1)}, u32[]{:S(2)}, u32[]{:S(2)}) collective-permute-start(f32[128,256]{1,0:T(8,128)S(1)} %get-tuple-element.111), channel_id=1, source_target_pairs={{0,1},{1,2},{2,3},{3,0},{4,5},{5,6},{6,7},{7,4},{8,9},{9,10},{10,1... | collective-permute-start | bytes 393224 | tf_op jit(solution)/shard_map/ppermute | solution.py:33
  9.4 6.2 %copy-start.1 = (bf16[512,8,512]{2,1,0:T(8,128)(2,1)S(1)}, bf16[512,8,512]{2,1,0:T(8,128)(2,1)}, u32[]{:S(2)}) copy-start(bf16[512,8,512]{2,1,0:T(8,128)(2,1)} %param.9) | copy-start | bytes 12582916
  9.9 7.6 %collective-permute-start.4 = (f32[128,256]{1,0:T(8,128)S(1)}, f32[128,256]{1,0:T(8,128)S(1)}, u32[]{:S(2)}, u32[]{:S(2)}) collective-permute-start(f32[128,256]{1,0:T(8,128)S(1)} %get-tuple-element.115), channel_id=1, source_target_pairs={{0,1},{1,2},{2,3},{3,0},{4,5},{5,6},{6,7},{7,4},{8,9},{9,10},{10,1... | collective-permute-start | bytes 393224 | tf_op jit(solution)/shard_map/ppermute | solution.py:33
  11.2 7.7 %collective-permute-start.5 = (f32[128,256]{1,0:T(8,128)S(1)}, f32[128,256]{1,0:T(8,128)S(1)}, u32[]{:S(2)}, u32[]{:S(2)}) collective-permute-start(f32[128,256]{1,0:T(8,128)S(1)} %get-tuple-element.120), channel_id=1, source_target_pairs={{0,1},{1,2},{2,3},{3,0},{4,5},{5,6},{6,7},{7,4},{8,9},{9,10},{10,1... | collective-permute-start | bytes 393224 | tf_op jit(solution)/shard_map/ppermute | solution.py:33
  12.8 2.8 %copy-start = (bf16[512,8,512]{2,1,0:T(8,128)(2,1)S(1)}, bf16[512,8,512]{2,1,0:T(8,128)(2,1)}, u32[]{:S(2)}) copy-start(bf16[512,8,512]{2,1,0:T(8,128)(2,1)} %param.8) | copy-start | bytes 12582916
  13.3 6.4 %collective-permute-start.6 = (f32[128,256]{1,0:T(8,128)S(1)}, f32[128,256]{1,0:T(8,128)S(1)}, u32[]{:S(2)}, u32[]{:S(2)}) collective-permute-start(f32[128,256]{1,0:T(8,128)S(1)} %get-tuple-element.122), channel_id=1, source_target_pairs={{0,1},{1,2},{2,3},{3,0},{4,5},{5,6},{6,7},{7,4},{8,9},{9,10},{10,1... | collective-permute-start | bytes 393224 | tf_op jit(solution)/shard_map/ppermute | solution.py:33
  14.7 5.8 %collective-permute-start.7 = (f32[128,256]{1,0:T(8,128)S(1)}, f32[128,256]{1,0:T(8,128)S(1)}, u32[]{:S(2)}, u32[]{:S(2)}) collective-permute-start(f32[128,256]{1,0:T(8,128)S(1)} %get-tuple-element.124), channel_id=1, source_target_pairs={{0,1},{1,2},{2,3},{3,0},{4,5},{5,6},{6,7},{7,4},{8,9},{9,10},{10,1... | collective-permute-start | bytes 393224 | tf_op jit(solution)/shard_map/ppermute | solution.py:33
  18.0 4.4 %collective-permute-start.8 = (f32[128,256]{1,0:T(8,128)S(1)}, f32[128,256]{1,0:T(8,128)S(1)}, u32[]{:S(2)}, u32[]{:S(2)}) collective-permute-start(f32[128,256]{1,0:T(8,128)S(1)} %get-tuple-element.128), channel_id=1, source_target_pairs={{0,1},{1,2},{2,3},{3,0},{4,5},{5,6},{6,7},{7,4},{8,9},{9,10},{10,1... | collective-permute-start | bytes 393224 | tf_op jit(solution)/shard_map/ppermute | solution.py:33
  19.4 5.0 %collective-permute-start.9 = (f32[128,256]{1,0:T(8,128)S(1)}, f32[128,256]{1,0:T(8,128)S(1)}, u32[]{:S(2)}, u32[]{:S(2)}) collective-permute-start(f32[128,256]{1,0:T(8,128)S(1)} %get-tuple-element.130), channel_id=1, source_target_pairs={{0,1},{1,2},{2,3},{3,0},{4,5},{5,6},{6,7},{7,4},{8,9},{9,10},{10,1... | collective-permute-start | bytes 393224 | tf_op jit(solution)/shard_map/ppermute | solution.py:33
  20.2 6.3 %collective-permute-start.10 = (f32[128,256]{1,0:T(8,128)S(1)}, f32[128,256]{1,0:T(8,128)S(1)}, u32[]{:S(2)}, u32[]{:S(2)}) collective-permute-start(f32[128,256]{1,0:T(8,128)S(1)} %get-tuple-element.132), channel_id=1, source_target_pairs={{0,1},{1,2},{2,3},{3,0},{4,5},{5,6},{6,7},{7,4},{8,9},{9,10},{10,1... | collective-permute-start | bytes 393224 | tf_op jit(solution)/shard_map/ppermute | solution.py:33
  20.9 7.6 %collective-permute-start.11 = (f32[128,256]{1,0:T(8,128)S(1)}, f32[128,256]{1,0:T(8,128)S(1)}, u32[]{:S(2)}, u32[]{:S(2)}) collective-permute-start(f32[128,256]{1,0:T(8,128)S(1)} %get-tuple-element.134), channel_id=1, source_target_pairs={{0,1},{1,2},{2,3},{3,0},{4,5},{5,6},{6,7},{7,4},{8,9},{9,10},{10,1... | collective-permute-start | bytes 393224 | tf_op jit(solution)/shard_map/ppermute | solution.py:33
  22.9 9.1 %collective-permute-start.12 = (f32[128,256]{1,0:T(8,128)S(1)}, f32[128,256]{1,0:T(8,128)S(1)}, u32[]{:S(2)}, u32[]{:S(2)}) collective-permute-start(f32[128,256]{1,0:T(8,128)S(1)} %get-tuple-element.138), channel_id=1, source_target_pairs={{0,4},{4,8},{8,12},{12,16},{16,20},{20,24},{24,28},{28,0},{1,5},{5... | collective-permute-start | bytes 393224 | tf_op jit(solution)/shard_map/ppermute | solution.py:33
  24.9 9.9 %collective-permute-start.13 = (f32[128,256]{1,0:T(8,128)S(1)}, f32[128,256]{1,0:T(8,128)S(1)}, u32[]{:S(2)}, u32[]{:S(2)}) collective-permute-start(f32[128,256]{1,0:T(8,128)S(1)} %get-tuple-element.140), channel_id=1, source_target_pairs={{0,4},{4,8},{8,12},{12,16},{16,20},{20,24},{24,28},{28,0},{1,5},{5... | collective-permute-start | bytes 393224 | tf_op jit(solution)/shard_map/ppermute | solution.py:33
  27.0 10.7 %collective-permute-start.14 = (f32[128,256]{1,0:T(8,128)S(1)}, f32[128,256]{1,0:T(8,128)S(1)}, u32[]{:S(2)}, u32[]{:S(2)}) collective-permute-start(f32[128,256]{1,0:T(8,128)S(1)} %get-tuple-element.142), channel_id=1, source_target_pairs={{0,4},{4,8},{8,12},{12,16},{16,20},{20,24},{24,28},{28,0},{1,5},{5... | collective-permute-start | bytes 393224 | tf_op jit(solution)/shard_map/ppermute | solution.py:33
  29.0 11.3 %collective-permute-start.15 = (f32[128,256]{1,0:T(8,128)S(1)}, f32[128,256]{1,0:T(8,128)S(1)}, u32[]{:S(2)}, u32[]{:S(2)}) collective-permute-start(f32[128,256]{1,0:T(8,128)S(1)} %get-tuple-element.144), channel_id=1, source_target_pairs={{0,4},{4,8},{8,12},{12,16},{16,20},{20,24},{24,28},{28,0},{1,5},{5... | collective-permute-start | bytes 393224 | tf_op jit(solution)/shard_map/ppermute | solution.py:33
  32.5 10.5 %collective-permute-start.16 = (f32[128,256]{1,0:T(8,128)S(1)}, f32[128,256]{1,0:T(8,128)S(1)}, u32[]{:S(2)}, u32[]{:S(2)}) collective-permute-start(f32[128,256]{1,0:T(8,128)S(1)} %get-tuple-element.148), channel_id=1, source_target_pairs={{0,1},{1,2},{2,3},{3,0},{4,5},{5,6},{6,7},{7,4},{8,9},{9,10},{10,1... | collective-permute-start | bytes 393224 | tf_op jit(solution)/shard_map/ppermute | solution.py:33
  35.3 8.8 %collective-permute-start.17 = (f32[128,256]{1,0:T(8,128)S(1)}, f32[128,256]{1,0:T(8,128)S(1)}, u32[]{:S(2)}, u32[]{:S(2)}) collective-permute-start(f32[128,256]{1,0:T(8,128)S(1)} %get-tuple-element.152), channel_id=1, source_target_pairs={{0,1},{1,2},{2,3},{3,0},{4,5},{5,6},{6,7},{7,4},{8,9},{9,10},{10,1... | collective-permute-start | bytes 393224 | tf_op jit(solution)/shard_map/ppermute | solution.py:33
  38.1 6.5 %collective-permute-start.18 = (f32[128,256]{1,0:T(8,128)S(1)}, f32[128,256]{1,0:T(8,128)S(1)}, u32[]{:S(2)}, u32[]{:S(2)}) collective-permute-start(f32[128,256]{1,0:T(8,128)S(1)} %get-tuple-element.154), channel_id=1, source_target_pairs={{0,1},{1,2},{2,3},{3,0},{4,5},{5,6},{6,7},{7,4},{8,9},{9,10},{10,1... | collective-permute-start | bytes 393224 | tf_op jit(solution)/shard_map/ppermute | solution.py:33
  40.8 6.0 %collective-permute-start.19 = (f32[128,256]{1,0:T(8,128)S(1)}, f32[128,256]{1,0:T(8,128)S(1)}, u32[]{:S(2)}, u32[]{:S(2)}) collective-permute-start(f32[128,256]{1,0:T(8,128)S(1)} %get-tuple-element.156), channel_id=1, source_target_pairs={{0,1},{1,2},{2,3},{3,0},{4,5},{5,6},{6,7},{7,4},{8,9},{9,10},{10,1... | collective-permute-start | bytes 393224 | tf_op jit(solution)/shard_map/ppermute | solution.py:33
  43.4 4.4 %collective-permute-start.20 = (f32[128,256]{1,0:T(8,128)S(1)}, f32[128,256]{1,0:T(8,128)S(1)}, u32[]{:S(2)}, u32[]{:S(2)}) collective-permute-start(f32[128,256]{1,0:T(8,128)S(1)} %get-tuple-element.160), channel_id=1, source_target_pairs={{0,1},{1,2},{2,3},{3,0},{4,5},{5,6},{6,7},{7,4},{8,9},{9,10},{10,1... | collective-permute-start | bytes 393224 | tf_op jit(solution)/shard_map/ppermute | solution.py:33
  44.5 4.7 %collective-permute-start.21 = (f32[128,256]{1,0:T(8,128)S(1)}, f32[128,256]{1,0:T(8,128)S(1)}, u32[]{:S(2)}, u32[]{:S(2)}) collective-permute-start(f32[128,256]{1,0:T(8,128)S(1)} %get-tuple-element.162), channel_id=1, source_target_pairs={{0,1},{1,2},{2,3},{3,0},{4,5},{5,6},{6,7},{7,4},{8,9},{9,10},{10,1... | collective-permute-start | bytes 393224 | tf_op jit(solution)/shard_map/ppermute | solution.py:33
  45.1 5.6 %collective-permute-start.22 = (f32[128,256]{1,0:T(8,128)S(1)}, f32[128,256]{1,0:T(8,128)S(1)}, u32[]{:S(2)}, u32[]{:S(2)}) collective-permute-start(f32[128,256]{1,0:T(8,128)S(1)} %get-tuple-element.164), channel_id=1, source_target_pairs={{0,1},{1,2},{2,3},{3,0},{4,5},{5,6},{6,7},{7,4},{8,9},{9,10},{10,1... | collective-permute-start | bytes 393224 | tf_op jit(solution)/shard_map/ppermute | solution.py:33
  47.2 4.9 %collective-permute-start.23 = (f32[128,256]{1,0:T(8,128)S(1)}, f32[128,256]{1,0:T(8,128)S(1)}, u32[]{:S(2)}, u32[]{:S(2)}) collective-permute-start(f32[128,256]{1,0:T(8,128)S(1)} %get-tuple-element.166), channel_id=1, source_target_pairs={{0,1},{1,2},{2,3},{3,0},{4,5},{5,6},{6,7},{7,4},{8,9},{9,10},{10,1... | collective-permute-start | bytes 393224 | tf_op jit(solution)/shard_map/ppermute | solution.py:33
  48.3 5.2 %collective-permute-start.26 = (f32[128,256]{1,0:T(8,128)S(1)}, f32[128,256]{1,0:T(8,128)S(1)}, u32[]{:S(2)}, u32[]{:S(2)}) collective-permute-start(f32[128,256]{1,0:T(8,128)S(1)} %get-tuple-element.172), channel_id=1, source_target_pairs={{0,1},{1,2},{2,3},{3,0},{4,5},{5,6},{6,7},{7,4},{8,9},{9,10},{10,1... | collective-permute-start | bytes 393224 | tf_op jit(solution)/shard_map/ppermute | solution.py:33
  49.7 5.2 %collective-permute-start.25 = (f32[128,256]{1,0:T(8,128)S(1)}, f32[128,256]{1,0:T(8,128)S(1)}, u32[]{:S(2)}, u32[]{:S(2)}) collective-permute-start(f32[128,256]{1,0:T(8,128)S(1)} %get-tuple-element.171), channel_id=1, source_target_pairs={{0,1},{1,2},{2,3},{3,0},{4,5},{5,6},{6,7},{7,4},{8,9},{9,10},{10,1... | collective-permute-start | bytes 393224 | tf_op jit(solution)/shard_map/ppermute | solution.py:33
  51.1 5.2 %collective-permute-start.24 = (f32[128,256]{1,0:T(8,128)S(1)}, f32[128,256]{1,0:T(8,128)S(1)}, u32[]{:S(2)}, u32[]{:S(2)}) collective-permute-start(f32[128,256]{1,0:T(8,128)S(1)} %get-tuple-element.170), channel_id=1, source_target_pairs={{0,1},{1,2},{2,3},{3,0},{4,5},{5,6},{6,7},{7,4},{8,9},{9,10},{10,1... | collective-permute-start | bytes 393224 | tf_op jit(solution)/shard_map/ppermute | solution.py:33
  52.5 5.2 %collective-permute-start.27 = (f32[128,256]{1,0:T(8,128)S(1)}, f32[128,256]{1,0:T(8,128)S(1)}, u32[]{:S(2)}, u32[]{:S(2)}) collective-permute-start(f32[128,256]{1,0:T(8,128)S(1)} %get-tuple-element.176), channel_id=1, source_target_pairs={{0,1},{1,2},{2,3},{3,0},{4,5},{5,6},{6,7},{7,4},{8,9},{9,10},{10,1... | collective-permute-start | bytes 393224 | tf_op jit(solution)/shard_map/ppermute | solution.py:33

commit v2 on v1

--- a/solution.py
+++ b/solution.py
@@ -77,7 +77,7 @@
 
     def kernel(
         list_hbm, count_hbm, user_hbm, item_hbm, rating_hbm, weight_hbm,
-        rating_out, weight_out, mask_out, user_out, half_out, *refs,
+        rating_out, weight_out, mask_out, user_out, half_out, new_out, residual_out, *refs,
     ):
         pieces, (raw, lists, counts, sems, small) = refs[:count], refs[count:]
         tables = [
@@ -91,11 +91,12 @@
         copies = [
             [
                 pltpu.make_async_copy(source.at[:, block, 0], raw.at[side, block], sems.at[side, block])
-                for block in range(blocks)
+                for side, source in enumerate((rating_hbm, weight_hbm))
             ]
-            for side, source in enumerate((rating_hbm, weight_hbm))
+            for block in range(blocks)
         ]
-        for copy in tables + copies[0] + copies[1] + factors:
+        ahead = sizes[0] // LANES
+        for copy in tables + sum(copies[:ahead], []) + factors[:2] + sum(copies[ahead:], []) + factors[2:]:
             copy.start()
         target = lax.broadcasted_iota(jnp.int32, (2 * GROUP, 2 * GROUP), 0)
         source = lax.broadcasted_iota(jnp.int32, (2 * GROUP, 2 * GROUP), 1)
@@ -110,22 +111,33 @@
                     hit = (lists[slot, stratum] == tile) & (slot < counts[0, stratum])
                     listed = jnp.where(hit, 1.0, listed)
                 mask_out[stratum : stratum + 1, tile * width : (tile + 1) * width] = jnp.full((1, width), listed)
-        for side, out in enumerate((rating_out, weight_out)):
-            for copy in copies[side]:
-                copy.wait()
-            for block in range(blocks):
-                pairs = raw.at[side, block].reshape(2 * users, LANES)
+
+        def sort(some):
+            for block in some:
+                for copy in copies[block]:
+                    copy.wait()
+            for block in some:
                 cols = slice(block * LANES, (block + 1) * LANES)
-                for first in range(0, users, GROUP):
-                    rows = jnp.dot(pick, pairs[2 * first : 2 * (first + GROUP), :], preferred_element_type=f32)
-                    for stratum in range(2):
-                        part = rows[stratum * GROUP : (stratum + 1) * GROUP]
-                        if side == 1:
-                            part = part * mask_out[stratum : stratum + 1, cols]
-                        out[stratum, first : first + GROUP, cols] = part.astype(bf16)
-        for copy in factors:
+                for side, out in enumerate((rating_out, weight_out)):
+                    pairs = raw.at[side, block].reshape(2 * users, LANES)
+                    for first in range(0, users, GROUP):
+                        rows = jnp.dot(pick, pairs[2 * first : 2 * (first + GROUP), :], preferred_element_type=f32)
+                        for stratum in range(2):
+                            part = rows[stratum * GROUP : (stratum + 1) * GROUP]
+                            if side == 1:
+                                part = part * mask_out[stratum : stratum + 1, cols]
+                            out[stratum, first : first + GROUP, cols] = part.astype(bf16)
+
+        sort(range(ahead))
+        for copy in factors[:2]:
             copy.wait()
         half_out[...] = user_out[...].astype(bf16)
+        residual_out[...], new_out[...] = piece_step(
+            half_out[...], pieces[0][...], rating_out, weight_out, 0, slice(0, sizes[0])
+        )
+        sort(range(ahead, blocks))
+        for copy in factors[2:]:
+            copy.wait()
 
     table = jax.ShapeDtypeStruct((2, users, items), bf16)
     outs = call(
@@ -136,10 +148,12 @@
             jax.ShapeDtypeStruct((strata, items), f32),
             jax.ShapeDtypeStruct((users, rank), f32),
             jax.ShapeDtypeStruct((users, rank), bf16),
+            jax.ShapeDtypeStruct((sizes[0], rank), f32),
+            jax.ShapeDtypeStruct((users, sizes[0]), bf16),
             *[jax.ShapeDtypeStruct((size, rank), f32) for size in sizes],
         ),
         [HBM] * 6,
-        (VMEM,) * (5 + count),
+        (VMEM,) * (7 + count),
         8 * users * items * GROUP,
         [
             pltpu.VMEM((2, blocks, users, 2, LANES), bf16),
@@ -152,7 +166,7 @@
         hbm(tile_list[0].T), hbm(tile_count), hbm(user_factors), hbm(item_factors),
         hbm(view(ratings)), hbm(view(weights)),
     )
-    return *outs[:5], list(outs[5:])
+    return *outs[:7], list(outs[7:])
 
 
 def sort_strata(chosen, ratings, weights, mask):
@@ -274,10 +288,21 @@
             write(new_ref, items_out.at[pl.ds(start, new_ref.shape[0])])
             start += new_ref.shape[0]
         rows = piece_ref[...]
-        residual, new_rows = piece_step(half_ref[...], rows, rating_ref, weight_ref, stratum, cols)
-        last_users[...] = user_ref[...] - learn_rate * (grad_ref[...] + users_grad(residual, rows))
-        write(last_users, users_out)
-        last_items[...] = new_rows
+        residuals = []
+        for part in range(2):
+            mine = slice(part * users // 2, (part + 1) * users // 2)
+            predicted = lax.dot_general(half_ref[mine, :], rows.astype(bf16), RANK, preferred_element_type=f32)
+            rating = rating_ref[stratum, mine, cols].astype(f32)
+            weight = weight_ref[stratum, mine, cols].astype(f32)
+            residuals.append((weight * (predicted - rating)).astype(bf16))
+            last_users[mine, :] = user_ref[mine, :] - learn_rate * (
+                grad_ref[mine, :] + users_grad(residuals[-1], rows)
+            )
+            span = pl.ds(part * users // 2, users // 2)
+            write(last_users.at[span], users_out.at[span])
+        residual = jnp.concatenate(residuals, axis=0)
+        grad = lax.dot_general(residual, half_ref[...], USERS, preferred_element_type=f32)
+        last_items[...] = rows - learn_rate * (grad + ridge_weight * rows)
         write(last_items, items_out.at[pl.ds(start, m)])
         for copy in copies:
             copy.wait()
@@ -292,7 +317,7 @@
         [
             pltpu.VMEM((m, rank), f32),
             pltpu.VMEM((users, rank), f32),
-            pltpu.SemaphoreType.DMA((done + 2,)),
+            pltpu.SemaphoreType.DMA((done + 3,)),
         ],
     )(user_rows, user_half, grad, piece, ratings, weights, *news)
 
@@ -301,7 +326,7 @@
     starts, sizes = cut(item_factors.shape[0])
     cols = [slice(start, start + size) for start, size in zip(starts, sizes)]
     last = len(sizes) - 1
-    rating_01, weight_01, mask, user_rows, user_half, pieces = load(
+    rating_01, weight_01, mask, user_rows, user_half, *opened, pieces = load(
         user_factors, item_factors, ratings, weights, tile_list, tile_count
     )
     tables = [(0, rating_01, weight_01), (1, rating_01, weight_01)]
@@ -328,7 +353,10 @@
                     earlier = (grad,)
                 return finish(row, cols[last], user_rows, user_half, grad, pieces[last], rating, weight, news)
             for j in range(last + 1):
-                new, residual = first_piece(row, cols[j], user_half, pieces[j], rating, weight)
+                if stratum == 0 and j == 0:
+                    new, residual = opened
+                else:
+                    new, residual = first_piece(row, cols[j], user_half, pieces[j], rating, weight)
                 residuals.append(residual)
                 news.append(move(new))
             user_rows, user_half = users_step(user_rows, residuals, pieces)

time: 59.5 us -> 59.1 us (level)
    pallas_call x29 -> x28, Pallas kernels: 13.2 us -> 12.8 us  [first_piece(): call(kernel, (jax.ShapeDtypeStruct((m, rank), f32), jax.ShapeDtypeStruct(...]
where the time goes in v2:
time: 59.1 us; the launch traced here: 59 us
  Pallas kernels  24.6 us (42%)
  starting transfers between devices  20.1 us (34%)
  waiting for transfers between devices  13 us (22%)
  between operations  1.19 us (2%)
    ppermute x28, starting transfers between devices, from_behind(): return lax.ppermute(value, axis, pairs)  20.1 us
    ppermute x28, waiting for transfers between devices, from_behind(): return lax.ppermute(value, axis, pairs)  13 us
    pallas_call x28, Pallas kernels, first_piece(): call(kernel, (jax.ShapeDtypeStruct((m, rank), f32), jax.ShapeDtypeStruct(...  12.8 us
    pallas_call x1, Pallas kernels, load(): call(kernel, (table, table, jax.ShapeDtypeStruct((strata, items), f32), j...  3.35 us
    pallas_call x7, Pallas kernels, users_step(): call(kernel, (jax.ShapeDtypeStruct((users, rank), f32), jax.ShapeDtypeStr...  2.97 us
    pallas_call x2, Pallas kernels, sort_strata(): call(kernel, (table, table), [VMEM] * 3, (VMEM, VMEM), 4 * kept * users *...  2.93 us
    pallas_call x1, Pallas kernels, finish(): call(kernel, (jax.ShapeDtypeStruct((users, rank), f32), jax.ShapeDtypeStr...  1.33 us
    pallas_call x2, Pallas kernels, middle_piece(): call(kernel, (jax.ShapeDtypeStruct((m, rank), f32), jax.ShapeDtypeStruct(...  1.27 us
  transfers between devices with their start and end apart: 28, of which 13 were waited for; matrix products, arithmetic and copies ran while one was open for 0% of the time, Pallas kernels for 34%

profile of v2, /device:TPU:0, one launch (start us, length us, event | category | flops | bytes accessed | tf_op | source)
XLA Modules:
  0.0 59.0 jit_solution(8241647645342984961)
XLA Ops:
  0.6 3.4 %shard_map.77 = (bf16[2,512,512]{2,1,0:T(8,128)(2,1)S(1)}, bf16[2,512,512]{2,1,0:T(8,128)(2,1)S(1)}, f32[8,512]{1,0:T(8,128)S(1)}, f32[512,256]{1,0:T(8,128)S(1)...) custom-call(s32[4,8]{1,0:T(4,128)} %bitcast.21, ...), custom_call_target="tpu_custom_call" | custom-call | flops 268435456 | bytes 1024 | tf_op jit(solution)/shard_map/pallas_call | solution.py:143
  4.0 0.5 collective-permute-start
  5.0 2.7 %collective-permute-start.1 = (f32[128,256]{1,0:T(8,128)S(1)}, f32[128,256]{1,0:T(8,128)S(1)}, u32[]{:S(2)}, u32[]{:S(2)}) collective-permute-start(f32[128,256]{1,0:T(8,128)S(1)} %get-tuple-element.107), channel_id=1, source_target_pairs={{0,1},{1,2},{2,3},{3,0},{4,5},{5,6},{6,7},{7,4},{8,9},{9,10},{10,1... | collective-permute-start | bytes 393224 | tf_op jit(solution)/shard_map/ppermute | solution.py:33
  9.7 0.8 %collective-permute-done.1.piece_ref.refs_5_ = f32[128,256]{1,0:T(8,128)S(1)} collective-permute-done((f32[128,256]{1,0:T(8,128)S(1)}, f32[128,256]{1,0:T(8,128)S(1)}, u32[]{:S(2)}, u32[]{:S(2)}) %collective-permute-start.1) | collective-permute-done | bytes 131104 | tf_op jit(solution)/shard_map/ppermute | solution.py:33
  11.0 1.6 %collective-permute-start.5 = (f32[128,256]{1,0:T(8,128)S(1)}, f32[128,256]{1,0:T(8,128)S(1)}, u32[]{:S(2)}, u32[]{:S(2)}) collective-permute-start(f32[128,256]{1,0:T(8,128)S(1)} %get-tuple-element.120), channel_id=1, source_target_pairs={{0,1},{1,2},{2,3},{3,0},{4,5},{5,6},{6,7},{7,4},{8,9},{9,10},{10,1... | collective-permute-start | bytes 393224 | tf_op jit(solution)/shard_map/ppermute | solution.py:33
  13.0 0.9 %collective-permute-start.6 = (f32[128,256]{1,0:T(8,128)S(1)}, f32[128,256]{1,0:T(8,128)S(1)}, u32[]{:S(2)}, u32[]{:S(2)}) collective-permute-start(f32[128,256]{1,0:T(8,128)S(1)} %get-tuple-element.122), channel_id=1, source_target_pairs={{0,1},{1,2},{2,3},{3,0},{4,5},{5,6},{6,7},{7,4},{8,9},{9,10},{10,1... | collective-permute-start | bytes 393224 | tf_op jit(solution)/shard_map/ppermute | solution.py:33
  14.4 0.9 %collective-permute-start.7 = (f32[128,256]{1,0:T(8,128)S(1)}, f32[128,256]{1,0:T(8,128)S(1)}, u32[]{:S(2)}, u32[]{:S(2)}) collective-permute-start(f32[128,256]{1,0:T(8,128)S(1)} %get-tuple-element.124), channel_id=1, source_target_pairs={{0,1},{1,2},{2,3},{3,0},{4,5},{5,6},{6,7},{7,4},{8,9},{9,10},{10,1... | collective-permute-start | bytes 393224 | tf_op jit(solution)/shard_map/ppermute | solution.py:33
  15.4 1.5 %shard_map.87 = (bf16[3,512,512]{2,1,0:T(8,128)(2,1)S(1)}, bf16[3,512,512]{2,1,0:T(8,128)(2,1)S(1)}) custom-call(bf16[4096,512]{1,0:T(8,128)(2,1)S(1)} %bitcast.16, bf16[4096,512]{1,0:T(8,128)(2,1)S(1)} %bitcast.19, f32[8,512]{1,0:T(8,128)S(1)} %get-tuple-element.116.mask_ref), custom_call_target="tpu_custom_call" | custom-call | flops 805306368 | bytes 1024 | tf_op jit(solution)/shard_map/pallas_call | solution.py:193
  17.3 0.5 shard_map.88
  17.8 0.9 %collective-permute-start.8 = (f32[128,256]{1,0:T(8,128)S(1)}, f32[128,256]{1,0:T(8,128)S(1)}, u32[]{:S(2)}, u32[]{:S(2)}) collective-permute-start(f32[128,256]{1,0:T(8,128)S(1)} %get-tuple-element.128), channel_id=1, source_target_pairs={{0,1},{1,2},{2,3},{3,0},{4,5},{5,6},{6,7},{7,4},{8,9},{9,10},{10,1... | collective-permute-start | bytes 393224 | tf_op jit(solution)/shard_map/ppermute | solution.py:33
  20.7 0.9 %collective-permute-start.11 = (f32[128,256]{1,0:T(8,128)S(1)}, f32[128,256]{1,0:T(8,128)S(1)}, u32[]{:S(2)}, u32[]{:S(2)}) collective-permute-start(f32[128,256]{1,0:T(8,128)S(1)} %get-tuple-element.134), channel_id=1, source_target_pairs={{0,1},{1,2},{2,3},{3,0},{4,5},{5,6},{6,7},{7,4},{8,9},{9,10},{10,1... | collective-permute-start | bytes 393224 | tf_op jit(solution)/shard_map/ppermute | solution.py:33
  22.7 1.5 %collective-permute-start.12 = (f32[128,256]{1,0:T(8,128)S(1)}, f32[128,256]{1,0:T(8,128)S(1)}, u32[]{:S(2)}, u32[]{:S(2)}) collective-permute-start(f32[128,256]{1,0:T(8,128)S(1)} %get-tuple-element.138), channel_id=1, source_target_pairs={{0,4},{4,8},{8,12},{12,16},{16,20},{20,24},{24,28},{28,0},{1,5},{5... | collective-permute-start | bytes 393224 | tf_op jit(solution)/shard_map/ppermute | solution.py:33
  24.7 1.6 %collective-permute-start.13 = (f32[128,256]{1,0:T(8,128)S(1)}, f32[128,256]{1,0:T(8,128)S(1)}, u32[]{:S(2)}, u32[]{:S(2)}) collective-permute-start(f32[128,256]{1,0:T(8,128)S(1)} %get-tuple-element.140), channel_id=1, source_target_pairs={{0,4},{4,8},{8,12},{12,16},{16,20},{20,24},{24,28},{28,0},{1,5},{5... | collective-permute-start | bytes 393224 | tf_op jit(solution)/shard_map/ppermute | solution.py:33
  26.8 1.5 %collective-permute-start.14 = (f32[128,256]{1,0:T(8,128)S(1)}, f32[128,256]{1,0:T(8,128)S(1)}, u32[]{:S(2)}, u32[]{:S(2)}) collective-permute-start(f32[128,256]{1,0:T(8,128)S(1)} %get-tuple-element.142), channel_id=1, source_target_pairs={{0,4},{4,8},{8,12},{12,16},{16,20},{20,24},{24,28},{28,0},{1,5},{5... | collective-permute-start | bytes 393224 | tf_op jit(solution)/shard_map/ppermute | solution.py:33
  28.8 1.6 %collective-permute-start.15 = (f32[128,256]{1,0:T(8,128)S(1)}, f32[128,256]{1,0:T(8,128)S(1)}, u32[]{:S(2)}, u32[]{:S(2)}) collective-permute-start(f32[128,256]{1,0:T(8,128)S(1)} %get-tuple-element.144), channel_id=1, source_target_pairs={{0,4},{4,8},{8,12},{12,16},{16,20},{20,24},{24,28},{28,0},{1,5},{5... | collective-permute-start | bytes 393224 | tf_op jit(solution)/shard_map/ppermute | solution.py:33
  30.8 1.0 %collective-permute-done.12.piece_ref.refs_4_ = f32[128,256]{1,0:T(8,128)S(1)} collective-permute-done((f32[128,256]{1,0:T(8,128)S(1)}, f32[128,256]{1,0:T(8,128)S(1)}, u32[]{:S(2)}, u32[]{:S(2)}) %collective-permute-start.12) | collective-permute-done | bytes 131104 | tf_op jit(solution)/shard_map/ppermute | solution.py:33
  32.3 2.3 %collective-permute-done.13.piece_ref.refs_5_ = f32[128,256]{1,0:T(8,128)S(1)} collective-permute-done((f32[128,256]{1,0:T(8,128)S(1)}, f32[128,256]{1,0:T(8,128)S(1)}, u32[]{:S(2)}, u32[]{:S(2)}) %collective-permute-start.13) | collective-permute-done | bytes 131104 | tf_op jit(solution)/shard_map/ppermute | solution.py:33
  35.1 2.3 %collective-permute-done.14.piece_ref.refs_6_ = f32[128,256]{1,0:T(8,128)S(1)} collective-permute-done((f32[128,256]{1,0:T(8,128)S(1)}, f32[128,256]{1,0:T(8,128)S(1)}, u32[]{:S(2)}, u32[]{:S(2)}) %collective-permute-start.14) | collective-permute-done | bytes 131104 | tf_op jit(solution)/shard_map/ppermute | solution.py:33
  37.9 2.2 %collective-permute-done.15.piece_ref.refs_7_ = f32[128,256]{1,0:T(8,128)S(1)} collective-permute-done((f32[128,256]{1,0:T(8,128)S(1)}, f32[128,256]{1,0:T(8,128)S(1)}, u32[]{:S(2)}, u32[]{:S(2)}) %collective-permute-start.15) | collective-permute-done | bytes 131104 | tf_op jit(solution)/shard_map/ppermute | solution.py:33
  40.8 1.5 %shard_map.103 = (bf16[3,512,512]{2,1,0:T(8,128)(2,1)S(1)}, bf16[3,512,512]{2,1,0:T(8,128)(2,1)S(1)}) custom-call(bf16[4096,512]{1,0:T(8,128)(2,1)S(1)} %bitcast.17, bf16[4096,512]{1,0:T(8,128)(2,1)S(1)} %bitcast.20, f32[8,512]{1,0:T(8,128)S(1)} %get-tuple-element.116.mask_ref), custom_call_target="tpu_custom_call" | custom-call | flops 805306368 | bytes 1024 | tf_op jit(solution)/shard_map/pallas_call | solution.py:193
  43.2 0.7 %collective-permute-start.20 = (f32[128,256]{1,0:T(8,128)S(1)}, f32[128,256]{1,0:T(8,128)S(1)}, u32[]{:S(2)}, u32[]{:S(2)}) collective-permute-start(f32[128,256]{1,0:T(8,128)S(1)} %get-tuple-element.160), channel_id=1, source_target_pairs={{0,1},{1,2},{2,3},{3,0},{4,5},{5,6},{6,7},{7,4},{8,9},{9,10},{10,1... | collective-permute-start | bytes 393224 | tf_op jit(solution)/shard_map/ppermute | solution.py:33
  44.9 1.7 %collective-permute-start.22 = (f32[128,256]{1,0:T(8,128)S(1)}, f32[128,256]{1,0:T(8,128)S(1)}, u32[]{:S(2)}, u32[]{:S(2)}) collective-permute-start(f32[128,256]{1,0:T(8,128)S(1)} %get-tuple-element.164), channel_id=1, source_target_pairs={{0,1},{1,2},{2,3},{3,0},{4,5},{5,6},{6,7},{7,4},{8,9},{9,10},{10,1... | collective-permute-start | bytes 393224 | tf_op jit(solution)/shard_map/ppermute | solution.py:33
  48.1 0.5 collective-permute-start.26
  49.6 0.9 %collective-permute-done.22.piece_ref.refs_6_ = f32[128,256]{1,0:T(8,128)S(1)} collective-permute-done((f32[128,256]{1,0:T(8,128)S(1)}, f32[128,256]{1,0:T(8,128)S(1)}, u32[]{:S(2)}, u32[]{:S(2)}) %collective-permute-start.22) | collective-permute-done | bytes 131104 | tf_op jit(solution)/shard_map/ppermute | solution.py:33
  50.9 0.5 collective-permute-start.24
  52.3 0.5 collective-permute-start.27
  53.7 0.9 %collective-permute-done.25.piece_ref = f32[128,256]{1,0:T(8,128)S(1)} collective-permute-done((f32[128,256]{1,0:T(8,128)S(1)}, f32[128,256]{1,0:T(8,128)S(1)}, u32[]{:S(2)}, u32[]{:S(2)}) %collective-permute-start.25) | collective-permute-done | bytes 131104 | tf_op jit(solution)/shard_map/ppermute | solution.py:33
  54.7 0.7 %shard_map.115 = (f32[128,256]{1,0:T(8,128)S(1)}, f32[512,256]{1,0:T(8,128)S(1)}) custom-call(f32[512,256]{1,0:T(8,128)S(1)} %get-tuple-element.168.user_ref, bf16[512,256]{1,0:T(8,128)(2,1)S(1)} %get-tuple-element.169.half_ref, f32[128,256]{1,0:T(8,128)S(1)} %collective-permute-done.25.piece_ref, bf16[3,512,512]{2,1,0:T(8,128)(2,1)S(1)} %get-tuple-element.149.rating_ref, ...), custom_call_target="tpu_custom_call" | custom-call | flops 134217728 | bytes 1024 | tf_op jit(solution)/shard_map/pallas_call | solution.py:264
  55.3 0.7 %collective-permute-done.24.piece_ref = f32[128,256]{1,0:T(8,128)S(1)} collective-permute-done((f32[128,256]{1,0:T(8,128)S(1)}, f32[128,256]{1,0:T(8,128)S(1)}, u32[]{:S(2)}, u32[]{:S(2)}) %collective-permute-start.24) | collective-permute-done | bytes 131104 | tf_op jit(solution)/shard_map/ppermute | solution.py:33
  56.1 0.6 %shard_map.116 = (f32[128,256]{1,0:T(8,128)S(1)}, f32[512,256]{1,0:T(8,128)S(1)}) custom-call(f32[512,256]{1,0:T(8,128)S(1)} %get-tuple-element.168.user_ref, bf16[512,256]{1,0:T(8,128)(2,1)S(1)} %get-tuple-element.169.half_ref, f32[128,256]{1,0:T(8,128)S(1)} %collective-permute-done.24.piece_ref, bf16[3,512,512]{2,1,0:T(8,128)(2,1)S(1)} %get-tuple-element.149.rating_ref, ...), custom_call_target="tpu_custom_call" | custom-call | flops 134217728 | bytes 1024 | tf_op jit(solution)/shard_map/pallas_call | solution.py:264
  56.7 0.8 %collective-permute-done.27.piece_ref = f32[128,256]{1,0:T(8,128)S(1)} collective-permute-done((f32[128,256]{1,0:T(8,128)S(1)}, f32[128,256]{1,0:T(8,128)S(1)}, u32[]{:S(2)}, u32[]{:S(2)}) %collective-permute-start.27) | collective-permute-done | bytes 131104 | tf_op jit(solution)/shard_map/ppermute | solution.py:33
  57.5 1.3 %shard_map.117 = (f32[512,256]{1,0:T(8,128)}, f32[512,256]{1,0:T(8,128)}) custom-call(f32[512,256]{1,0:T(8,128)S(1)} %get-tuple-element.168.user_ref, bf16[512,256]{1,0:T(8,128)(2,1)S(1)} %get-tuple-element.169.half_ref, f32[512,256]{1,0:T(8,128)S(1)} %get-tuple-element.175.grad_ref, f32[128,256]{1,0:T(8,128)S(1)} %collective-permute-done.27.piece_ref, ...), custom_call_target="tpu_custom_call" | custom-call | flops 100663296 | bytes 1024 | tf_op jit(solution)/shard_map/pallas_call | solution.py:311
  (69 shorter events, 17.9 us)
Async XLA Ops:
  4.0 5.2 %collective-permute-start = (f32[128,256]{1,0:T(8,128)S(1)}, f32[128,256]{1,0:T(8,128)S(1)}, u32[]{:S(2)}, u32[]{:S(2)}) collective-permute-start(f32[128,256]{1,0:T(8,128)S(1)} %get-tuple-element.105), channel_id=1, source_target_pairs={{0,1},{1,2},{2,3},{3,0},{4,5},{5,6},{6,7},{7,4},{8,9},{9,10},{10,1... | collective-permute-start | bytes 393224 | tf_op jit(solution)/shard_map/ppermute | solution.py:33
  5.0 5.5 %collective-permute-start.1 = (f32[128,256]{1,0:T(8,128)S(1)}, f32[128,256]{1,0:T(8,128)S(1)}, u32[]{:S(2)}, u32[]{:S(2)}) collective-permute-start(f32[128,256]{1,0:T(8,128)S(1)} %get-tuple-element.107), channel_id=1, source_target_pairs={{0,1},{1,2},{2,3},{3,0},{4,5},{5,6},{6,7},{7,4},{8,9},{9,10},{10,1... | collective-permute-start | bytes 393224 | tf_op jit(solution)/shard_map/ppermute | solution.py:33
  8.1 4.5 %collective-permute-start.2 = (f32[128,256]{1,0:T(8,128)S(1)}, f32[128,256]{1,0:T(8,128)S(1)}, u32[]{:S(2)}, u32[]{:S(2)}) collective-permute-start(f32[128,256]{1,0:T(8,128)S(1)} %get-tuple-element.109), channel_id=1, source_target_pairs={{0,1},{1,2},{2,3},{3,0},{4,5},{5,6},{6,7},{7,4},{8,9},{9,10},{10,1... | collective-permute-start | bytes 393224 | tf_op jit(solution)/shard_map/ppermute | solution.py:33
  8.7 5.3 %collective-permute-start.3 = (f32[128,256]{1,0:T(8,128)S(1)}, f32[128,256]{1,0:T(8,128)S(1)}, u32[]{:S(2)}, u32[]{:S(2)}) collective-permute-start(f32[128,256]{1,0:T(8,128)S(1)} %get-tuple-element.111), channel_id=1, source_target_pairs={{0,1},{1,2},{2,3},{3,0},{4,5},{5,6},{6,7},{7,4},{8,9},{9,10},{10,1... | collective-permute-start | bytes 393224 | tf_op jit(solution)/shard_map/ppermute | solution.py:33
  9.2 6.2 %copy-start.1 = (bf16[512,8,512]{2,1,0:T(8,128)(2,1)S(1)}, bf16[512,8,512]{2,1,0:T(8,128)(2,1)}, u32[]{:S(2)}) copy-start(bf16[512,8,512]{2,1,0:T(8,128)(2,1)} %param.9) | copy-start | bytes 12582916
  9.6 7.6 %collective-permute-start.4 = (f32[128,256]{1,0:T(8,128)S(1)}, f32[128,256]{1,0:T(8,128)S(1)}, u32[]{:S(2)}, u32[]{:S(2)}) collective-permute-start(f32[128,256]{1,0:T(8,128)S(1)} %get-tuple-element.115), channel_id=1, source_target_pairs={{0,1},{1,2},{2,3},{3,0},{4,5},{5,6},{6,7},{7,4},{8,9},{9,10},{10,1... | collective-permute-start | bytes 393224 | tf_op jit(solution)/shard_map/ppermute | solution.py:33
  11.0 7.7 %collective-permute-start.5 = (f32[128,256]{1,0:T(8,128)S(1)}, f32[128,256]{1,0:T(8,128)S(1)}, u32[]{:S(2)}, u32[]{:S(2)}) collective-permute-start(f32[128,256]{1,0:T(8,128)S(1)} %get-tuple-element.120), channel_id=1, source_target_pairs={{0,1},{1,2},{2,3},{3,0},{4,5},{5,6},{6,7},{7,4},{8,9},{9,10},{10,1... | collective-permute-start | bytes 393224 | tf_op jit(solution)/shard_map/ppermute | solution.py:33
  12.6 2.8 %copy-start = (bf16[512,8,512]{2,1,0:T(8,128)(2,1)S(1)}, bf16[512,8,512]{2,1,0:T(8,128)(2,1)}, u32[]{:S(2)}) copy-start(bf16[512,8,512]{2,1,0:T(8,128)(2,1)} %param.8) | copy-start | bytes 12582916
  13.0 6.4 %collective-permute-start.6 = (f32[128,256]{1,0:T(8,128)S(1)}, f32[128,256]{1,0:T(8,128)S(1)}, u32[]{:S(2)}, u32[]{:S(2)}) collective-permute-start(f32[128,256]{1,0:T(8,128)S(1)} %get-tuple-element.122), channel_id=1, source_target_pairs={{0,1},{1,2},{2,3},{3,0},{4,5},{5,6},{6,7},{7,4},{8,9},{9,10},{10,1... | collective-permute-start | bytes 393224 | tf_op jit(solution)/shard_map/ppermute | solution.py:33
  14.4 5.8 %collective-permute-start.7 = (f32[128,256]{1,0:T(8,128)S(1)}, f32[128,256]{1,0:T(8,128)S(1)}, u32[]{:S(2)}, u32[]{:S(2)}) collective-permute-start(f32[128,256]{1,0:T(8,128)S(1)} %get-tuple-element.124), channel_id=1, source_target_pairs={{0,1},{1,2},{2,3},{3,0},{4,5},{5,6},{6,7},{7,4},{8,9},{9,10},{10,1... | collective-permute-start | bytes 393224 | tf_op jit(solution)/shard_map/ppermute | solution.py:33
  17.8 4.4 %collective-permute-start.8 = (f32[128,256]{1,0:T(8,128)S(1)}, f32[128,256]{1,0:T(8,128)S(1)}, u32[]{:S(2)}, u32[]{:S(2)}) collective-permute-start(f32[128,256]{1,0:T(8,128)S(1)} %get-tuple-element.128), channel_id=1, source_target_pairs={{0,1},{1,2},{2,3},{3,0},{4,5},{5,6},{6,7},{7,4},{8,9},{9,10},{10,1... | collective-permute-start | bytes 393224 | tf_op jit(solution)/shard_map/ppermute | solution.py:33
  19.2 5.1 %collective-permute-start.9 = (f32[128,256]{1,0:T(8,128)S(1)}, f32[128,256]{1,0:T(8,128)S(1)}, u32[]{:S(2)}, u32[]{:S(2)}) collective-permute-start(f32[128,256]{1,0:T(8,128)S(1)} %get-tuple-element.130), channel_id=1, source_target_pairs={{0,1},{1,2},{2,3},{3,0},{4,5},{5,6},{6,7},{7,4},{8,9},{9,10},{10,1... | collective-permute-start | bytes 393224 | tf_op jit(solution)/shard_map/ppermute | solution.py:33
  20.0 6.3 %collective-permute-start.10 = (f32[128,256]{1,0:T(8,128)S(1)}, f32[128,256]{1,0:T(8,128)S(1)}, u32[]{:S(2)}, u32[]{:S(2)}) collective-permute-start(f32[128,256]{1,0:T(8,128)S(1)} %get-tuple-element.132), channel_id=1, source_target_pairs={{0,1},{1,2},{2,3},{3,0},{4,5},{5,6},{6,7},{7,4},{8,9},{9,10},{10,1... | collective-permute-start | bytes 393224 | tf_op jit(solution)/shard_map/ppermute | solution.py:33
  20.7 7.6 %collective-permute-start.11 = (f32[128,256]{1,0:T(8,128)S(1)}, f32[128,256]{1,0:T(8,128)S(1)}, u32[]{:S(2)}, u32[]{:S(2)}) collective-permute-start(f32[128,256]{1,0:T(8,128)S(1)} %get-tuple-element.134), channel_id=1, source_target_pairs={{0,1},{1,2},{2,3},{3,0},{4,5},{5,6},{6,7},{7,4},{8,9},{9,10},{10,1... | collective-permute-start | bytes 393224 | tf_op jit(solution)/shard_map/ppermute | solution.py:33
  22.7 9.1 %collective-permute-start.12 = (f32[128,256]{1,0:T(8,128)S(1)}, f32[128,256]{1,0:T(8,128)S(1)}, u32[]{:S(2)}, u32[]{:S(2)}) collective-permute-start(f32[128,256]{1,0:T(8,128)S(1)} %get-tuple-element.138), channel_id=1, source_target_pairs={{0,4},{4,8},{8,12},{12,16},{16,20},{20,24},{24,28},{28,0},{1,5},{5... | collective-permute-start | bytes 393224 | tf_op jit(solution)/shard_map/ppermute | solution.py:33
  24.7 9.9 %collective-permute-start.13 = (f32[128,256]{1,0:T(8,128)S(1)}, f32[128,256]{1,0:T(8,128)S(1)}, u32[]{:S(2)}, u32[]{:S(2)}) collective-permute-start(f32[128,256]{1,0:T(8,128)S(1)} %get-tuple-element.140), channel_id=1, source_target_pairs={{0,4},{4,8},{8,12},{12,16},{16,20},{20,24},{24,28},{28,0},{1,5},{5... | collective-permute-start | bytes 393224 | tf_op jit(solution)/shard_map/ppermute | solution.py:33
  26.8 10.6 %collective-permute-start.14 = (f32[128,256]{1,0:T(8,128)S(1)}, f32[128,256]{1,0:T(8,128)S(1)}, u32[]{:S(2)}, u32[]{:S(2)}) collective-permute-start(f32[128,256]{1,0:T(8,128)S(1)} %get-tuple-element.142), channel_id=1, source_target_pairs={{0,4},{4,8},{8,12},{12,16},{16,20},{20,24},{24,28},{28,0},{1,5},{5... | collective-permute-start | bytes 393224 | tf_op jit(solution)/shard_map/ppermute | solution.py:33
  28.8 11.3 %collective-permute-start.15 = (f32[128,256]{1,0:T(8,128)S(1)}, f32[128,256]{1,0:T(8,128)S(1)}, u32[]{:S(2)}, u32[]{:S(2)}) collective-permute-start(f32[128,256]{1,0:T(8,128)S(1)} %get-tuple-element.144), channel_id=1, source_target_pairs={{0,4},{4,8},{8,12},{12,16},{16,20},{20,24},{24,28},{28,0},{1,5},{5... | collective-permute-start | bytes 393224 | tf_op jit(solution)/shard_map/ppermute | solution.py:33
  32.3 10.5 %collective-permute-start.16 = (f32[128,256]{1,0:T(8,128)S(1)}, f32[128,256]{1,0:T(8,128)S(1)}, u32[]{:S(2)}, u32[]{:S(2)}) collective-permute-start(f32[128,256]{1,0:T(8,128)S(1)} %get-tuple-element.148), channel_id=1, source_target_pairs={{0,1},{1,2},{2,3},{3,0},{4,5},{5,6},{6,7},{7,4},{8,9},{9,10},{10,1... | collective-permute-start | bytes 393224 | tf_op jit(solution)/shard_map/ppermute | solution.py:33
  35.1 8.8 %collective-permute-start.17 = (f32[128,256]{1,0:T(8,128)S(1)}, f32[128,256]{1,0:T(8,128)S(1)}, u32[]{:S(2)}, u32[]{:S(2)}) collective-permute-start(f32[128,256]{1,0:T(8,128)S(1)} %get-tuple-element.152), channel_id=1, source_target_pairs={{0,1},{1,2},{2,3},{3,0},{4,5},{5,6},{6,7},{7,4},{8,9},{9,10},{10,1... | collective-permute-start | bytes 393224 | tf_op jit(solution)/shard_map/ppermute | solution.py:33
  37.9 6.5 %collective-permute-start.18 = (f32[128,256]{1,0:T(8,128)S(1)}, f32[128,256]{1,0:T(8,128)S(1)}, u32[]{:S(2)}, u32[]{:S(2)}) collective-permute-start(f32[128,256]{1,0:T(8,128)S(1)} %get-tuple-element.154), channel_id=1, source_target_pairs={{0,1},{1,2},{2,3},{3,0},{4,5},{5,6},{6,7},{7,4},{8,9},{9,10},{10,1... | collective-permute-start | bytes 393224 | tf_op jit(solution)/shard_map/ppermute | solution.py:33
  40.6 6.0 %collective-permute-start.19 = (f32[128,256]{1,0:T(8,128)S(1)}, f32[128,256]{1,0:T(8,128)S(1)}, u32[]{:S(2)}, u32[]{:S(2)}) collective-permute-start(f32[128,256]{1,0:T(8,128)S(1)} %get-tuple-element.156), channel_id=1, source_target_pairs={{0,1},{1,2},{2,3},{3,0},{4,5},{5,6},{6,7},{7,4},{8,9},{9,10},{10,1... | collective-permute-start | bytes 393224 | tf_op jit(solution)/shard_map/ppermute | solution.py:33
  43.2 4.4 %collective-permute-start.20 = (f32[128,256]{1,0:T(8,128)S(1)}, f32[128,256]{1,0:T(8,128)S(1)}, u32[]{:S(2)}, u32[]{:S(2)}) collective-permute-start(f32[128,256]{1,0:T(8,128)S(1)} %get-tuple-element.160), channel_id=1, source_target_pairs={{0,1},{1,2},{2,3},{3,0},{4,5},{5,6},{6,7},{7,4},{8,9},{9,10},{10,1... | collective-permute-start | bytes 393224 | tf_op jit(solution)/shard_map/ppermute | solution.py:33
  44.3 4.7 %collective-permute-start.21 = (f32[128,256]{1,0:T(8,128)S(1)}, f32[128,256]{1,0:T(8,128)S(1)}, u32[]{:S(2)}, u32[]{:S(2)}) collective-permute-start(f32[128,256]{1,0:T(8,128)S(1)} %get-tuple-element.162), channel_id=1, source_target_pairs={{0,1},{1,2},{2,3},{3,0},{4,5},{5,6},{6,7},{7,4},{8,9},{9,10},{10,1... | collective-permute-start | bytes 393224 | tf_op jit(solution)/shard_map/ppermute | solution.py:33
  44.9 5.6 %collective-permute-start.22 = (f32[128,256]{1,0:T(8,128)S(1)}, f32[128,256]{1,0:T(8,128)S(1)}, u32[]{:S(2)}, u32[]{:S(2)}) collective-permute-start(f32[128,256]{1,0:T(8,128)S(1)} %get-tuple-element.164), channel_id=1, source_target_pairs={{0,1},{1,2},{2,3},{3,0},{4,5},{5,6},{6,7},{7,4},{8,9},{9,10},{10,1... | collective-permute-start | bytes 393224 | tf_op jit(solution)/shard_map/ppermute | solution.py:33
  47.0 4.9 %collective-permute-start.23 = (f32[128,256]{1,0:T(8,128)S(1)}, f32[128,256]{1,0:T(8,128)S(1)}, u32[]{:S(2)}, u32[]{:S(2)}) collective-permute-start(f32[128,256]{1,0:T(8,128)S(1)} %get-tuple-element.166), channel_id=1, source_target_pairs={{0,1},{1,2},{2,3},{3,0},{4,5},{5,6},{6,7},{7,4},{8,9},{9,10},{10,1... | collective-permute-start | bytes 393224 | tf_op jit(solution)/shard_map/ppermute | solution.py:33
  48.1 5.2 %collective-permute-start.26 = (f32[128,256]{1,0:T(8,128)S(1)}, f32[128,256]{1,0:T(8,128)S(1)}, u32[]{:S(2)}, u32[]{:S(2)}) collective-permute-start(f32[128,256]{1,0:T(8,128)S(1)} %get-tuple-element.172), channel_id=1, source_target_pairs={{0,1},{1,2},{2,3},{3,0},{4,5},{5,6},{6,7},{7,4},{8,9},{9,10},{10,1... | collective-permute-start | bytes 393224 | tf_op jit(solution)/shard_map/ppermute | solution.py:33
  49.5 5.2 %collective-permute-start.25 = (f32[128,256]{1,0:T(8,128)S(1)}, f32[128,256]{1,0:T(8,128)S(1)}, u32[]{:S(2)}, u32[]{:S(2)}) collective-permute-start(f32[128,256]{1,0:T(8,128)S(1)} %get-tuple-element.171), channel_id=1, source_target_pairs={{0,1},{1,2},{2,3},{3,0},{4,5},{5,6},{6,7},{7,4},{8,9},{9,10},{10,1... | collective-permute-start | bytes 393224 | tf_op jit(solution)/shard_map/ppermute | solution.py:33
  50.9 5.2 %collective-permute-start.24 = (f32[128,256]{1,0:T(8,128)S(1)}, f32[128,256]{1,0:T(8,128)S(1)}, u32[]{:S(2)}, u32[]{:S(2)}) collective-permute-start(f32[128,256]{1,0:T(8,128)S(1)} %get-tuple-element.170), channel_id=1, source_target_pairs={{0,1},{1,2},{2,3},{3,0},{4,5},{5,6},{6,7},{7,4},{8,9},{9,10},{10,1... | collective-permute-start | bytes 393224 | tf_op jit(solution)/shard_map/ppermute | solution.py:33
  52.3 5.2 %collective-permute-start.27 = (f32[128,256]{1,0:T(8,128)S(1)}, f32[128,256]{1,0:T(8,128)S(1)}, u32[]{:S(2)}, u32[]{:S(2)}) collective-permute-start(f32[128,256]{1,0:T(8,128)S(1)} %get-tuple-element.176), channel_id=1, source_target_pairs={{0,1},{1,2},{2,3},{3,0},{4,5},{5,6},{6,7},{7,4},{8,9},{9,10},{10,1... | collective-permute-start | bytes 393224 | tf_op jit(solution)/shard_map/ppermute | solution.py:33

commit v3 on v2

--- a/solution.py
+++ b/solution.py
@@ -9,7 +9,7 @@
 S_OUT = 2
 S_IN = 4
 SHARES = (1, 1, 1, 1)
-LATER = ((2, 3, 4), (5, 6, 7))
+LATER = ((2, 3), (4, 5, 6, 7))
 CHUNK = 32
 GROUP = 128
 LANES = 128
@@ -60,6 +60,44 @@
 
 def hbm(value):
     return pltpu.with_memory_space_constraint(value, pltpu.HBM)
+
+
+def sort_pairs(some, raw, mask, rating_out, weight_out):
+    users = rating_out.shape[1]
+    target = lax.broadcasted_iota(jnp.int32, (2 * GROUP, 2 * GROUP), 0)
+    source = lax.broadcasted_iota(jnp.int32, (2 * GROUP, 2 * GROUP), 1)
+    wanted = (target % GROUP) * 2 + target // GROUP
+    pick = jnp.where(source == wanted, 1.0, 0.0).astype(bf16)
+    for block in some:
+        cols = slice(block * LANES, (block + 1) * LANES)
+        for side, out in enumerate((rating_out, weight_out)):
+            pairs = raw.at[side, block].reshape(2 * users, LANES)
+            for first in range(0, users, GROUP):
+                rows = jnp.dot(pick, pairs[2 * first : 2 * (first + GROUP), :], preferred_element_type=f32)
+                for stratum in range(2):
+                    part = rows[stratum * GROUP : (stratum + 1) * GROUP]
+                    if side == 1:
+                        part = part * mask[stratum : stratum + 1, cols]
+                    out[stratum, first : first + GROUP, cols] = part.astype(bf16)
+
+
+def sort_rest(raw, mask, ratings, weights, ahead, after):
+    def kernel(raw_ref, mask_ref, rating_in, weight_in, after_ref, rating_out, weight_out):
+        @pl.when(lax.axis_index("inner") % 2 == 0)
+        def _():
+            sort_pairs(range(ahead, raw_ref.shape[1]), raw_ref, mask_ref, rating_out, weight_out)
+
+    table = jax.ShapeDtypeStruct(ratings.shape, bf16)
+    return pl.pallas_call(
+        kernel,
+        out_shape=(table, table),
+        in_specs=[VMEM] * 4 + [pl.BlockSpec(memory_space=pl.ANY)],
+        out_specs=(VMEM, VMEM),
+        input_output_aliases={2: 0, 3: 1},
+        compiler_params=pltpu.CompilerParams(vmem_limit_bytes=LIMIT),
+        cost_estimate=pl.CostEstimate(flops=1024, bytes_accessed=1024, transcendentals=0),
+        name="sort_rest",
+    )(raw, mask, ratings, weights, after)
 
 
 def load(user_factors, item_factors, ratings, weights, tile_list, tile_count):
@@ -77,9 +115,9 @@
 
     def kernel(
         list_hbm, count_hbm, user_hbm, item_hbm, rating_hbm, weight_hbm,
-        rating_out, weight_out, mask_out, user_out, half_out, new_out, residual_out, *refs,
+        rating_out, weight_out, mask_out, user_out, half_out, new_out, residual_out, raw, *refs,
     ):
-        pieces, (raw, lists, counts, sems, small) = refs[:count], refs[count:]
+        pieces, (lists, counts, sems, small) = refs[:count], refs[count:]
         tables = [
             pltpu.make_async_copy(list_hbm, lists, small.at[0]),
             pltpu.make_async_copy(count_hbm, counts, small.at[1]),
@@ -98,10 +136,6 @@
         ahead = sizes[0] // LANES
         for copy in tables + sum(copies[:ahead], []) + factors[:2] + sum(copies[ahead:], []) + factors[2:]:
             copy.start()
-        target = lax.broadcasted_iota(jnp.int32, (2 * GROUP, 2 * GROUP), 0)
-        source = lax.broadcasted_iota(jnp.int32, (2 * GROUP, 2 * GROUP), 1)
-        wanted = (target % GROUP) * 2 + target // GROUP
-        pick = jnp.where(source == wanted, 1.0, 0.0).astype(bf16)
         for copy in tables:
             copy.wait()
         for stratum in range(strata):
@@ -112,32 +146,23 @@
                     listed = jnp.where(hit, 1.0, listed)
                 mask_out[stratum : stratum + 1, tile * width : (tile + 1) * width] = jnp.full((1, width), listed)
 
-        def sort(some):
-            for block in some:
-                for copy in copies[block]:
-                    copy.wait()
-            for block in some:
-                cols = slice(block * LANES, (block + 1) * LANES)
-                for side, out in enumerate((rating_out, weight_out)):
-                    pairs = raw.at[side, block].reshape(2 * users, LANES)
-                    for first in range(0, users, GROUP):
-                        rows = jnp.dot(pick, pairs[2 * first : 2 * (first + GROUP), :], preferred_element_type=f32)
-                        for stratum in range(2):
-                            part = rows[stratum * GROUP : (stratum + 1) * GROUP]
-                            if side == 1:
-                                part = part * mask_out[stratum : stratum + 1, cols]
-                            out[stratum, first : first + GROUP, cols] = part.astype(bf16)
-
-        sort(range(ahead))
+        for copy in sum(copies[:ahead], []):
+            copy.wait()
+        sort_pairs(range(ahead), raw, mask_out, rating_out, weight_out)
         for copy in factors[:2]:
             copy.wait()
         half_out[...] = user_out[...].astype(bf16)
         residual_out[...], new_out[...] = piece_step(
             half_out[...], pieces[0][...], rating_out, weight_out, 0, slice(0, sizes[0])
         )
-        sort(range(ahead, blocks))
-        for copy in factors[2:]:
+        for copy in sum(copies[ahead:], []) + factors[2:]:
             copy.wait()
+
+        sort_pairs(range(ahead, 2 * ahead), raw, mask_out, rating_out, weight_out)
+
+        @pl.when(lax.axis_index("inner") % 2 == 1)
+        def _():
+            sort_pairs(range(2 * ahead, blocks), raw, mask_out, rating_out, weight_out)
 
     table = jax.ShapeDtypeStruct((2, users, items), bf16)
     outs = call(
@@ -150,13 +175,13 @@
             jax.ShapeDtypeStruct((users, rank), bf16),
             jax.ShapeDtypeStruct((sizes[0], rank), f32),
             jax.ShapeDtypeStruct((users, sizes[0]), bf16),
+            jax.ShapeDtypeStruct((2, blocks, users, 2, LANES), bf16),
             *[jax.ShapeDtypeStruct((size, rank), f32) for size in sizes],
         ),
         [HBM] * 6,
-        (VMEM,) * (7 + count),
+        (VMEM,) * (8 + count),
         8 * users * items * GROUP,
         [
-            pltpu.VMEM((2, blocks, users, 2, LANES), bf16),
             pltpu.SMEM((tiles, strata), jnp.int32),
             pltpu.SMEM((1, strata), jnp.int32),
             pltpu.SemaphoreType.DMA((2, blocks)),
@@ -166,7 +191,7 @@
         hbm(tile_list[0].T), hbm(tile_count), hbm(user_factors), hbm(item_factors),
         hbm(view(ratings)), hbm(view(weights)),
     )
-    return *outs[:7], list(outs[7:])
+    return *outs[:8], list(outs[8:])
 
 
 def sort_strata(chosen, ratings, weights, mask):
@@ -326,7 +351,7 @@
     starts, sizes = cut(item_factors.shape[0])
     cols = [slice(start, start + size) for start, size in zip(starts, sizes)]
     last = len(sizes) - 1
-    rating_01, weight_01, mask, user_rows, user_half, *opened, pieces = load(
+    rating_01, weight_01, mask, user_rows, user_half, *opened, raw, pieces = load(
         user_factors, item_factors, ratings, weights, tile_list, tile_count
     )
     tables = [(0, rating_01, weight_01), (1, rating_01, weight_01)]
@@ -359,6 +384,9 @@
                     new, residual = first_piece(row, cols[j], user_half, pieces[j], rating, weight)
                 residuals.append(residual)
                 news.append(move(new))
+                if stratum == 0 and j == 1:
+                    rating, weight = sort_rest(raw, mask, rating, weight, 2 * sizes[0] // LANES, residual)
+                    tables[:2] = [(0, rating, weight), (1, rating, weight)]
             user_rows, user_half = users_step(user_rows, residuals, pieces)
             pieces = news
 

time: 59.1 us -> 58.7 us (level)
  waiting for transfers between devices: 13 us -> 12.4 us
    pallas_call x0 -> x1, Pallas kernels: none -> 0.85 us  [sort_rest(): pl.pallas_call(kernel, out_shape=(table, table), in_specs=[VMEM] * 4 + [p...]
    pallas_call x1, Pallas kernels: 3.35 us -> 2.66 us  [load(): call(kernel, (table, table, jax.ShapeDtypeStruct((strata, items), f32), j...]
  transfers between devices with their start and end apart: 28 -> 28, of which waited for: 13 -> 13; matrix products, arithmetic and copies ran while one was open for 0% -> 0% of each run, Pallas kernels for 34% -> 35%
where the time goes in v3:
time: 58.7 us; the launch traced here: 58.6 us
  Pallas kernels  24.7 us (42%)
  starting transfers between devices  20.2 us (34%)
  waiting for transfers between devices  12.4 us (21%)
  between operations  1.22 us (2%)
    ppermute x28, starting transfers between devices, from_behind(): return lax.ppermute(value, axis, pairs)  20.2 us
    pallas_call x28, Pallas kernels, first_piece(): call(kernel, (jax.ShapeDtypeStruct((m, rank), f32), jax.ShapeDtypeStruct(...  12.8 us
    ppermute x28, waiting for transfers between devices, from_behind(): return lax.ppermute(value, axis, pairs)  12.4 us
    pallas_call x7, Pallas kernels, users_step(): call(kernel, (jax.ShapeDtypeStruct((users, rank), f32), jax.ShapeDtypeStr...  2.96 us
    pallas_call x2, Pallas kernels, sort_strata(): call(kernel, (table, table), [VMEM] * 3, (VMEM, VMEM), 4 * kept * users *...  2.83 us
    pallas_call x1, Pallas kernels, load(): call(kernel, (table, table, jax.ShapeDtypeStruct((strata, items), f32), j...  2.66 us
    pallas_call x1, Pallas kernels, finish(): call(kernel, (jax.ShapeDtypeStruct((users, rank), f32), jax.ShapeDtypeStr...  1.33 us
    pallas_call x2, Pallas kernels, middle_piece(): call(kernel, (jax.ShapeDtypeStruct((m, rank), f32), jax.ShapeDtypeStruct(...  1.27 us
  transfers between devices with their start and end apart: 28, of which 13 were waited for; matrix products, arithmetic and copies ran while one was open for 0% of the time, Pallas kernels for 35%

profile of v3, /device:TPU:0, one launch (start us, length us, event | category | flops | bytes accessed | tf_op | source)
XLA Modules:
  0.0 58.6 jit_solution(16277110889400431929)
XLA Ops:
  0.6 2.7 %shard_map.77 = (bf16[2,512,512]{2,1,0:T(8,128)(2,1)S(1)}, bf16[2,512,512]{2,1,0:T(8,128)(2,1)S(1)}, f32[8,512]{1,0:T(8,128)S(1)}, f32[512,256]{1,0:T(8,128)S(1)...) custom-call(s32[4,8]{1,0:T(4,128)} %bitcast.21, ...), custom_call_target="tpu_custom_call" | custom-call | flops 268435456 | bytes 1024 | tf_op jit(solution)/shard_map/pallas_call | solution.py:168
  3.3 1.4 %collective-permute-start = (f32[128,256]{1,0:T(8,128)S(1)}, f32[128,256]{1,0:T(8,128)S(1)}, u32[]{:S(2)}, u32[]{:S(2)}) collective-permute-start(f32[128,256]{1,0:T(8,128)S(1)} %get-tuple-element.112), channel_id=1, source_target_pairs={{0,1},{1,2},{2,3},{3,0},{4,5},{5,6},{6,7},{7,4},{8,9},{9,10},{10,1... | collective-permute-start | bytes 393224 | tf_op jit(solution)/shard_map/ppermute | solution.py:33
  5.1 1.9 %collective-permute-start.1 = (f32[128,256]{1,0:T(8,128)S(1)}, f32[128,256]{1,0:T(8,128)S(1)}, u32[]{:S(2)}, u32[]{:S(2)}) collective-permute-start(f32[128,256]{1,0:T(8,128)S(1)} %get-tuple-element.114), channel_id=1, source_target_pairs={{0,1},{1,2},{2,3},{3,0},{4,5},{5,6},{6,7},{7,4},{8,9},{9,10},{10,1... | collective-permute-start | bytes 393224 | tf_op jit(solution)/shard_map/ppermute | solution.py:33
  7.0 0.9 %sort_rest.1 = (bf16[2,512,512]{2,1,0:T(8,128)(2,1)S(1)}, bf16[2,512,512]{2,1,0:T(8,128)(2,1)S(1)}) custom-call(bf16[2,4,512,2,128]{4,3,2,1,0:T(2,128)(2,1)S(1)} %get-tuple-element.102.raw_ref, f32[8,512]{1,0:T(8,128)S(1)} %get-tuple-element.103.mask_ref, ...), custom_call_target="tpu_custom_call", output_to_operand_aliasing={{0}: (2, {}), {1}: (3, {})} | custom-call | flops 1024 | bytes 1024 | tf_op jit(solution)/shard_map/sort_rest/pallas_call | solution.py:91
  8.8 0.7 %collective-permute-start.2 = (f32[128,256]{1,0:T(8,128)S(1)}, f32[128,256]{1,0:T(8,128)S(1)}, u32[]{:S(2)}, u32[]{:S(2)}) collective-permute-start(f32[128,256]{1,0:T(8,128)S(1)} %get-tuple-element.116), channel_id=1, source_target_pairs={{0,1},{1,2},{2,3},{3,0},{4,5},{5,6},{6,7},{7,4},{8,9},{9,10},{10,1... | collective-permute-start | bytes 393224 | tf_op jit(solution)/shard_map/ppermute | solution.py:33
  11.1 1.5 %collective-permute-start.5 = (f32[128,256]{1,0:T(8,128)S(1)}, f32[128,256]{1,0:T(8,128)S(1)}, u32[]{:S(2)}, u32[]{:S(2)}) collective-permute-start(f32[128,256]{1,0:T(8,128)S(1)} %get-tuple-element.126), channel_id=1, source_target_pairs={{0,1},{1,2},{2,3},{3,0},{4,5},{5,6},{6,7},{7,4},{8,9},{9,10},{10,1... | collective-permute-start | bytes 393224 | tf_op jit(solution)/shard_map/ppermute | solution.py:33
  13.3 0.8 %collective-permute-done.2.piece_ref.refs_6_ = f32[128,256]{1,0:T(8,128)S(1)} collective-permute-done((f32[128,256]{1,0:T(8,128)S(1)}, f32[128,256]{1,0:T(8,128)S(1)}, u32[]{:S(2)}, u32[]{:S(2)}) %collective-permute-start.2) | collective-permute-done | bytes 131104 | tf_op jit(solution)/shard_map/ppermute | solution.py:33
  14.7 1.6 %shard_map.87 = (bf16[2,512,512]{2,1,0:T(8,128)(2,1)S(1)}, bf16[2,512,512]{2,1,0:T(8,128)(2,1)S(1)}) custom-call(bf16[4096,512]{1,0:T(8,128)(2,1)S(1)} %bitcast.16, bf16[4096,512]{1,0:T(8,128)(2,1)S(1)} %bitcast.19, f32[8,512]{1,0:T(8,128)S(1)} %get-tuple-element.103.mask_ref), custom_call_target="tpu_custom_call" | custom-call | flops 536870912 | bytes 1024 | tf_op jit(solution)/shard_map/pallas_call | solution.py:218
  17.2 0.9 %collective-permute-start.8 = (f32[128,256]{1,0:T(8,128)S(1)}, f32[128,256]{1,0:T(8,128)S(1)}, u32[]{:S(2)}, u32[]{:S(2)}) collective-permute-start(f32[128,256]{1,0:T(8,128)S(1)} %get-tuple-element.134), channel_id=1, source_target_pairs={{0,1},{1,2},{2,3},{3,0},{4,5},{5,6},{6,7},{7,4},{8,9},{9,10},{10,1... | collective-permute-start | bytes 393224 | tf_op jit(solution)/shard_map/ppermute | solution.py:33
  18.6 0.5 collective-permute-start.9
  19.6 0.9 %collective-permute-start.11 = (f32[128,256]{1,0:T(8,128)S(1)}, f32[128,256]{1,0:T(8,128)S(1)}, u32[]{:S(2)}, u32[]{:S(2)}) collective-permute-start(f32[128,256]{1,0:T(8,128)S(1)} %get-tuple-element.140), channel_id=1, source_target_pairs={{0,1},{1,2},{2,3},{3,0},{4,5},{5,6},{6,7},{7,4},{8,9},{9,10},{10,1... | collective-permute-start | bytes 393224 | tf_op jit(solution)/shard_map/ppermute | solution.py:33
  22.1 1.5 %collective-permute-start.12 = (f32[128,256]{1,0:T(8,128)S(1)}, f32[128,256]{1,0:T(8,128)S(1)}, u32[]{:S(2)}, u32[]{:S(2)}) collective-permute-start(f32[128,256]{1,0:T(8,128)S(1)} %get-tuple-element.144), channel_id=1, source_target_pairs={{0,4},{4,8},{8,12},{12,16},{16,20},{20,24},{24,28},{28,0},{1,5},{5... | collective-permute-start | bytes 393224 | tf_op jit(solution)/shard_map/ppermute | solution.py:33
  24.1 1.6 %collective-permute-start.13 = (f32[128,256]{1,0:T(8,128)S(1)}, f32[128,256]{1,0:T(8,128)S(1)}, u32[]{:S(2)}, u32[]{:S(2)}) collective-permute-start(f32[128,256]{1,0:T(8,128)S(1)} %get-tuple-element.148), channel_id=1, source_target_pairs={{0,4},{4,8},{8,12},{12,16},{16,20},{20,24},{24,28},{28,0},{1,5},{5... | collective-permute-start | bytes 393224 | tf_op jit(solution)/shard_map/ppermute | solution.py:33
  26.2 1.5 %collective-permute-start.15 = (f32[128,256]{1,0:T(8,128)S(1)}, f32[128,256]{1,0:T(8,128)S(1)}, u32[]{:S(2)}, u32[]{:S(2)}) collective-permute-start(f32[128,256]{1,0:T(8,128)S(1)} %get-tuple-element.152), channel_id=1, source_target_pairs={{0,4},{4,8},{8,12},{12,16},{16,20},{20,24},{24,28},{28,0},{1,5},{5... | collective-permute-start | bytes 393224 | tf_op jit(solution)/shard_map/ppermute | solution.py:33
  28.2 1.8 %collective-permute-start.14 = (f32[128,256]{1,0:T(8,128)S(1)}, f32[128,256]{1,0:T(8,128)S(1)}, u32[]{:S(2)}, u32[]{:S(2)}) collective-permute-start(f32[128,256]{1,0:T(8,128)S(1)} %get-tuple-element.150), channel_id=1, source_target_pairs={{0,4},{4,8},{8,12},{12,16},{16,20},{20,24},{24,28},{28,0},{1,5},{5... | collective-permute-start | bytes 393224 | tf_op jit(solution)/shard_map/ppermute | solution.py:33
  30.0 1.3 %shard_map.98 = (bf16[4,512,512]{2,1,0:T(8,128)(2,1)S(1)}, bf16[4,512,512]{2,1,0:T(8,128)(2,1)S(1)}) custom-call(bf16[4096,512]{1,0:T(8,128)(2,1)S(1)} %bitcast.17, bf16[4096,512]{1,0:T(8,128)(2,1)S(1)} %bitcast.20, f32[8,512]{1,0:T(8,128)S(1)} %get-tuple-element.103.mask_ref), custom_call_target="tpu_custom_call" | custom-call | flops 1073741824 | bytes 1024 | tf_op jit(solution)/shard_map/pallas_call | solution.py:218
  32.2 1.8 %collective-permute-done.13.piece_ref.refs_5_ = f32[128,256]{1,0:T(8,128)S(1)} collective-permute-done((f32[128,256]{1,0:T(8,128)S(1)}, f32[128,256]{1,0:T(8,128)S(1)}, u32[]{:S(2)}, u32[]{:S(2)}) %collective-permute-start.13) | collective-permute-done | bytes 131104 | tf_op jit(solution)/shard_map/ppermute | solution.py:33
  34.6 5.0 %collective-permute-done.14.piece_ref.refs_6_ = f32[128,256]{1,0:T(8,128)S(1)} collective-permute-done((f32[128,256]{1,0:T(8,128)S(1)}, f32[128,256]{1,0:T(8,128)S(1)}, u32[]{:S(2)}, u32[]{:S(2)}) %collective-permute-start.14) | collective-permute-done | bytes 131104 | tf_op jit(solution)/shard_map/ppermute | solution.py:33
  40.5 1.4 %collective-permute-start.19 = (f32[128,256]{1,0:T(8,128)S(1)}, f32[128,256]{1,0:T(8,128)S(1)}, u32[]{:S(2)}, u32[]{:S(2)}) collective-permute-start(f32[128,256]{1,0:T(8,128)S(1)} %get-tuple-element.162), channel_id=1, source_target_pairs={{0,1},{1,2},{2,3},{3,0},{4,5},{5,6},{6,7},{7,4},{8,9},{9,10},{10,1... | collective-permute-start | bytes 393224 | tf_op jit(solution)/shard_map/ppermute | solution.py:33
  43.3 0.9 %collective-permute-start.21 = (f32[128,256]{1,0:T(8,128)S(1)}, f32[128,256]{1,0:T(8,128)S(1)}, u32[]{:S(2)}, u32[]{:S(2)}) collective-permute-start(f32[128,256]{1,0:T(8,128)S(1)} %get-tuple-element.168), channel_id=1, source_target_pairs={{0,1},{1,2},{2,3},{3,0},{4,5},{5,6},{6,7},{7,4},{8,9},{9,10},{10,1... | collective-permute-start | bytes 393224 | tf_op jit(solution)/shard_map/ppermute | solution.py:33
  45.0 0.9 %collective-permute-done.19.piece_ref.refs_7_ = f32[128,256]{1,0:T(8,128)S(1)} collective-permute-done((f32[128,256]{1,0:T(8,128)S(1)}, f32[128,256]{1,0:T(8,128)S(1)}, u32[]{:S(2)}, u32[]{:S(2)}) %collective-permute-start.19) | collective-permute-done | bytes 131104 | tf_op jit(solution)/shard_map/ppermute | solution.py:33
  46.3 0.5 collective-permute-start.23
  47.7 0.9 %collective-permute-start.26 = (f32[128,256]{1,0:T(8,128)S(1)}, f32[128,256]{1,0:T(8,128)S(1)}, u32[]{:S(2)}, u32[]{:S(2)}) collective-permute-start(f32[128,256]{1,0:T(8,128)S(1)} %get-tuple-element.178), channel_id=1, source_target_pairs={{0,1},{1,2},{2,3},{3,0},{4,5},{5,6},{6,7},{7,4},{8,9},{9,10},{10,1... | collective-permute-start | bytes 393224 | tf_op jit(solution)/shard_map/ppermute | solution.py:33
  49.1 0.5 collective-permute-start.25
  50.5 0.5 collective-permute-start.24
  51.9 0.5 collective-permute-start.27
  53.3 0.9 %collective-permute-done.25.piece_ref = f32[128,256]{1,0:T(8,128)S(1)} collective-permute-done((f32[128,256]{1,0:T(8,128)S(1)}, f32[128,256]{1,0:T(8,128)S(1)}, u32[]{:S(2)}, u32[]{:S(2)}) %collective-permute-start.25) | collective-permute-done | bytes 131104 | tf_op jit(solution)/shard_map/ppermute | solution.py:33
  54.3 0.7 %shard_map.115 = (f32[128,256]{1,0:T(8,128)S(1)}, f32[512,256]{1,0:T(8,128)S(1)}) custom-call(f32[512,256]{1,0:T(8,128)S(1)} %get-tuple-element.174.user_ref, bf16[512,256]{1,0:T(8,128)(2,1)S(1)} %get-tuple-element.175.half_ref, f32[128,256]{1,0:T(8,128)S(1)} %collective-permute-done.25.piece_ref, bf16[4,512,512]{2,1,0:T(8,128)(2,1)S(1)} %get-tuple-element.145.rating_ref, ...), custom_call_target="tpu_custom_call" | custom-call | flops 134217728 | bytes 1024 | tf_op jit(solution)/shard_map/pallas_call | solution.py:289
  54.9 0.7 %collective-permute-done.24.piece_ref = f32[128,256]{1,0:T(8,128)S(1)} collective-permute-done((f32[128,256]{1,0:T(8,128)S(1)}, f32[128,256]{1,0:T(8,128)S(1)}, u32[]{:S(2)}, u32[]{:S(2)}) %collective-permute-start.24) | collective-permute-done | bytes 131104 | tf_op jit(solution)/shard_map/ppermute | solution.py:33
  55.7 0.6 %shard_map.116 = (f32[128,256]{1,0:T(8,128)S(1)}, f32[512,256]{1,0:T(8,128)S(1)}) custom-call(f32[512,256]{1,0:T(8,128)S(1)} %get-tuple-element.174.user_ref, bf16[512,256]{1,0:T(8,128)(2,1)S(1)} %get-tuple-element.175.half_ref, f32[128,256]{1,0:T(8,128)S(1)} %collective-permute-done.24.piece_ref, bf16[4,512,512]{2,1,0:T(8,128)(2,1)S(1)} %get-tuple-element.145.rating_ref, ...), custom_call_target="tpu_custom_call" | custom-call | flops 134217728 | bytes 1024 | tf_op jit(solution)/shard_map/pallas_call | solution.py:289
  56.3 0.8 %collective-permute-done.27.piece_ref = f32[128,256]{1,0:T(8,128)S(1)} collective-permute-done((f32[128,256]{1,0:T(8,128)S(1)}, f32[128,256]{1,0:T(8,128)S(1)}, u32[]{:S(2)}, u32[]{:S(2)}) %collective-permute-start.27) | collective-permute-done | bytes 131104 | tf_op jit(solution)/shard_map/ppermute | solution.py:33
  57.1 1.3 %shard_map.117 = (f32[512,256]{1,0:T(8,128)}, f32[512,256]{1,0:T(8,128)}) custom-call(f32[512,256]{1,0:T(8,128)S(1)} %get-tuple-element.174.user_ref, bf16[512,256]{1,0:T(8,128)(2,1)S(1)} %get-tuple-element.175.half_ref, f32[512,256]{1,0:T(8,128)S(1)} %get-tuple-element.181.grad_ref, f32[128,256]{1,0:T(8,128)S(1)} %collective-permute-done.27.piece_ref, ...), custom_call_target="tpu_custom_call" | custom-call | flops 100663296 | bytes 1024 | tf_op jit(solution)/shard_map/pallas_call | solution.py:336
  (70 shorter events, 17.9 us)
Async XLA Ops:
  3.3 6.7 %collective-permute-start = (f32[128,256]{1,0:T(8,128)S(1)}, f32[128,256]{1,0:T(8,128)S(1)}, u32[]{:S(2)}, u32[]{:S(2)}) collective-permute-start(f32[128,256]{1,0:T(8,128)S(1)} %get-tuple-element.112), channel_id=1, source_target_pairs={{0,1},{1,2},{2,3},{3,0},{4,5},{5,6},{6,7},{7,4},{8,9},{9,10},{10,1... | collective-permute-start | bytes 393224 | tf_op jit(solution)/shard_map/ppermute | solution.py:33
  5.1 5.5 %collective-permute-start.1 = (f32[128,256]{1,0:T(8,128)S(1)}, f32[128,256]{1,0:T(8,128)S(1)}, u32[]{:S(2)}, u32[]{:S(2)}) collective-permute-start(f32[128,256]{1,0:T(8,128)S(1)} %get-tuple-element.114), channel_id=1, source_target_pairs={{0,1},{1,2},{2,3},{3,0},{4,5},{5,6},{6,7},{7,4},{8,9},{9,10},{10,1... | collective-permute-start | bytes 393224 | tf_op jit(solution)/shard_map/ppermute | solution.py:33
  8.3 4.4 %collective-permute-start.3 = (f32[128,256]{1,0:T(8,128)S(1)}, f32[128,256]{1,0:T(8,128)S(1)}, u32[]{:S(2)}, u32[]{:S(2)}) collective-permute-start(f32[128,256]{1,0:T(8,128)S(1)} %get-tuple-element.118), channel_id=1, source_target_pairs={{0,1},{1,2},{2,3},{3,0},{4,5},{5,6},{6,7},{7,4},{8,9},{9,10},{10,1... | collective-permute-start | bytes 393224 | tf_op jit(solution)/shard_map/ppermute | solution.py:33
  8.8 5.3 %collective-permute-start.2 = (f32[128,256]{1,0:T(8,128)S(1)}, f32[128,256]{1,0:T(8,128)S(1)}, u32[]{:S(2)}, u32[]{:S(2)}) collective-permute-start(f32[128,256]{1,0:T(8,128)S(1)} %get-tuple-element.116), channel_id=1, source_target_pairs={{0,1},{1,2},{2,3},{3,0},{4,5},{5,6},{6,7},{7,4},{8,9},{9,10},{10,1... | collective-permute-start | bytes 393224 | tf_op jit(solution)/shard_map/ppermute | solution.py:33
  10.0 4.7 %copy-start.1 = (bf16[512,8,512]{2,1,0:T(8,128)(2,1)S(1)}, bf16[512,8,512]{2,1,0:T(8,128)(2,1)}, u32[]{:S(2)}) copy-start(bf16[512,8,512]{2,1,0:T(8,128)(2,1)} %param.9) | copy-start | bytes 12582916
  10.5 6.3 %collective-permute-start.4 = (f32[128,256]{1,0:T(8,128)S(1)}, f32[128,256]{1,0:T(8,128)S(1)}, u32[]{:S(2)}, u32[]{:S(2)}) collective-permute-start(f32[128,256]{1,0:T(8,128)S(1)} %get-tuple-element.122), channel_id=1, source_target_pairs={{0,1},{1,2},{2,3},{3,0},{4,5},{5,6},{6,7},{7,4},{8,9},{9,10},{10,1... | collective-permute-start | bytes 393224 | tf_op jit(solution)/shard_map/ppermute | solution.py:33
  11.1 3.6 %copy-start = (bf16[512,8,512]{2,1,0:T(8,128)(2,1)S(1)}, bf16[512,8,512]{2,1,0:T(8,128)(2,1)}, u32[]{:S(2)}) copy-start(bf16[512,8,512]{2,1,0:T(8,128)(2,1)} %param.8) | copy-start | bytes 12582916
  11.1 7.0 %collective-permute-start.5 = (f32[128,256]{1,0:T(8,128)S(1)}, f32[128,256]{1,0:T(8,128)S(1)}, u32[]{:S(2)}, u32[]{:S(2)}) collective-permute-start(f32[128,256]{1,0:T(8,128)S(1)} %get-tuple-element.126), channel_id=1, source_target_pairs={{0,1},{1,2},{2,3},{3,0},{4,5},{5,6},{6,7},{7,4},{8,9},{9,10},{10,1... | collective-permute-start | bytes 393224 | tf_op jit(solution)/shard_map/ppermute | solution.py:33
  13.2 5.9 %collective-permute-start.7 = (f32[128,256]{1,0:T(8,128)S(1)}, f32[128,256]{1,0:T(8,128)S(1)}, u32[]{:S(2)}, u32[]{:S(2)}) collective-permute-start(f32[128,256]{1,0:T(8,128)S(1)} %get-tuple-element.130), channel_id=1, source_target_pairs={{0,1},{1,2},{2,3},{3,0},{4,5},{5,6},{6,7},{7,4},{8,9},{9,10},{10,1... | collective-permute-start | bytes 393224 | tf_op jit(solution)/shard_map/ppermute | solution.py:33
  14.6 5.9 %collective-permute-start.6 = (f32[128,256]{1,0:T(8,128)S(1)}, f32[128,256]{1,0:T(8,128)S(1)}, u32[]{:S(2)}, u32[]{:S(2)}) collective-permute-start(f32[128,256]{1,0:T(8,128)S(1)} %get-tuple-element.128), channel_id=1, source_target_pairs={{0,1},{1,2},{2,3},{3,0},{4,5},{5,6},{6,7},{7,4},{8,9},{9,10},{10,1... | collective-permute-start | bytes 393224 | tf_op jit(solution)/shard_map/ppermute | solution.py:33
  17.2 4.4 %collective-permute-start.8 = (f32[128,256]{1,0:T(8,128)S(1)}, f32[128,256]{1,0:T(8,128)S(1)}, u32[]{:S(2)}, u32[]{:S(2)}) collective-permute-start(f32[128,256]{1,0:T(8,128)S(1)} %get-tuple-element.134), channel_id=1, source_target_pairs={{0,1},{1,2},{2,3},{3,0},{4,5},{5,6},{6,7},{7,4},{8,9},{9,10},{10,1... | collective-permute-start | bytes 393224 | tf_op jit(solution)/shard_map/ppermute | solution.py:33
  18.6 5.0 %collective-permute-start.9 = (f32[128,256]{1,0:T(8,128)S(1)}, f32[128,256]{1,0:T(8,128)S(1)}, u32[]{:S(2)}, u32[]{:S(2)}) collective-permute-start(f32[128,256]{1,0:T(8,128)S(1)} %get-tuple-element.136), channel_id=1, source_target_pairs={{0,1},{1,2},{2,3},{3,0},{4,5},{5,6},{6,7},{7,4},{8,9},{9,10},{10,1... | collective-permute-start | bytes 393224 | tf_op jit(solution)/shard_map/ppermute | solution.py:33
  19.6 6.1 %collective-permute-start.11 = (f32[128,256]{1,0:T(8,128)S(1)}, f32[128,256]{1,0:T(8,128)S(1)}, u32[]{:S(2)}, u32[]{:S(2)}) collective-permute-start(f32[128,256]{1,0:T(8,128)S(1)} %get-tuple-element.140), channel_id=1, source_target_pairs={{0,1},{1,2},{2,3},{3,0},{4,5},{5,6},{6,7},{7,4},{8,9},{9,10},{10,1... | collective-permute-start | bytes 393224 | tf_op jit(solution)/shard_map/ppermute | solution.py:33
  21.0 6.7 %collective-permute-start.10 = (f32[128,256]{1,0:T(8,128)S(1)}, f32[128,256]{1,0:T(8,128)S(1)}, u32[]{:S(2)}, u32[]{:S(2)}) collective-permute-start(f32[128,256]{1,0:T(8,128)S(1)} %get-tuple-element.138), channel_id=1, source_target_pairs={{0,1},{1,2},{2,3},{3,0},{4,5},{5,6},{6,7},{7,4},{8,9},{9,10},{10,1... | collective-permute-start | bytes 393224 | tf_op jit(solution)/shard_map/ppermute | solution.py:33
  22.1 9.6 %collective-permute-start.12 = (f32[128,256]{1,0:T(8,128)S(1)}, f32[128,256]{1,0:T(8,128)S(1)}, u32[]{:S(2)}, u32[]{:S(2)}) collective-permute-start(f32[128,256]{1,0:T(8,128)S(1)} %get-tuple-element.144), channel_id=1, source_target_pairs={{0,4},{4,8},{8,12},{12,16},{16,20},{20,24},{24,28},{28,0},{1,5},{5... | collective-permute-start | bytes 393224 | tf_op jit(solution)/shard_map/ppermute | solution.py:33
  24.1 9.9 %collective-permute-start.13 = (f32[128,256]{1,0:T(8,128)S(1)}, f32[128,256]{1,0:T(8,128)S(1)}, u32[]{:S(2)}, u32[]{:S(2)}) collective-permute-start(f32[128,256]{1,0:T(8,128)S(1)} %get-tuple-element.148), channel_id=1, source_target_pairs={{0,4},{4,8},{8,12},{12,16},{16,20},{20,24},{24,28},{28,0},{1,5},{5... | collective-permute-start | bytes 393224 | tf_op jit(solution)/shard_map/ppermute | solution.py:33
  26.2 13.9 %collective-permute-start.15 = (f32[128,256]{1,0:T(8,128)S(1)}, f32[128,256]{1,0:T(8,128)S(1)}, u32[]{:S(2)}, u32[]{:S(2)}) collective-permute-start(f32[128,256]{1,0:T(8,128)S(1)} %get-tuple-element.152), channel_id=1, source_target_pairs={{0,4},{4,8},{8,12},{12,16},{16,20},{20,24},{24,28},{28,0},{1,5},{5... | collective-permute-start | bytes 393224 | tf_op jit(solution)/shard_map/ppermute | solution.py:33
  28.2 11.3 %collective-permute-start.14 = (f32[128,256]{1,0:T(8,128)S(1)}, f32[128,256]{1,0:T(8,128)S(1)}, u32[]{:S(2)}, u32[]{:S(2)}) collective-permute-start(f32[128,256]{1,0:T(8,128)S(1)} %get-tuple-element.150), channel_id=1, source_target_pairs={{0,4},{4,8},{8,12},{12,16},{16,20},{20,24},{24,28},{28,0},{1,5},{5... | collective-permute-start | bytes 393224 | tf_op jit(solution)/shard_map/ppermute | solution.py:33
  32.1 10.2 %collective-permute-start.16 = (f32[128,256]{1,0:T(8,128)S(1)}, f32[128,256]{1,0:T(8,128)S(1)}, u32[]{:S(2)}, u32[]{:S(2)}) collective-permute-start(f32[128,256]{1,0:T(8,128)S(1)} %get-tuple-element.156), channel_id=1, source_target_pairs={{0,1},{1,2},{2,3},{3,0},{4,5},{5,6},{6,7},{7,4},{8,9},{9,10},{10,1... | collective-permute-start | bytes 393224 | tf_op jit(solution)/shard_map/ppermute | solution.py:33
  34.5 8.4 %collective-permute-start.17 = (f32[128,256]{1,0:T(8,128)S(1)}, f32[128,256]{1,0:T(8,128)S(1)}, u32[]{:S(2)}, u32[]{:S(2)}) collective-permute-start(f32[128,256]{1,0:T(8,128)S(1)} %get-tuple-element.158), channel_id=1, source_target_pairs={{0,1},{1,2},{2,3},{3,0},{4,5},{5,6},{6,7},{7,4},{8,9},{9,10},{10,1... | collective-permute-start | bytes 393224 | tf_op jit(solution)/shard_map/ppermute | solution.py:33
  40.0 4.4 %collective-permute-start.18 = (f32[128,256]{1,0:T(8,128)S(1)}, f32[128,256]{1,0:T(8,128)S(1)}, u32[]{:S(2)}, u32[]{:S(2)}) collective-permute-start(f32[128,256]{1,0:T(8,128)S(1)} %get-tuple-element.160), channel_id=1, source_target_pairs={{0,1},{1,2},{2,3},{3,0},{4,5},{5,6},{6,7},{7,4},{8,9},{9,10},{10,1... | collective-permute-start | bytes 393224 | tf_op jit(solution)/shard_map/ppermute | solution.py:33
  40.5 5.3 %collective-permute-start.19 = (f32[128,256]{1,0:T(8,128)S(1)}, f32[128,256]{1,0:T(8,128)S(1)}, u32[]{:S(2)}, u32[]{:S(2)}) collective-permute-start(f32[128,256]{1,0:T(8,128)S(1)} %get-tuple-element.162), channel_id=1, source_target_pairs={{0,1},{1,2},{2,3},{3,0},{4,5},{5,6},{6,7},{7,4},{8,9},{9,10},{10,1... | collective-permute-start | bytes 393224 | tf_op jit(solution)/shard_map/ppermute | solution.py:33
  42.8 4.4 %collective-permute-start.20 = (f32[128,256]{1,0:T(8,128)S(1)}, f32[128,256]{1,0:T(8,128)S(1)}, u32[]{:S(2)}, u32[]{:S(2)}) collective-permute-start(f32[128,256]{1,0:T(8,128)S(1)} %get-tuple-element.166), channel_id=1, source_target_pairs={{0,1},{1,2},{2,3},{3,0},{4,5},{5,6},{6,7},{7,4},{8,9},{9,10},{10,1... | collective-permute-start | bytes 393224 | tf_op jit(solution)/shard_map/ppermute | solution.py:33
  43.3 5.3 %collective-permute-start.21 = (f32[128,256]{1,0:T(8,128)S(1)}, f32[128,256]{1,0:T(8,128)S(1)}, u32[]{:S(2)}, u32[]{:S(2)}) collective-permute-start(f32[128,256]{1,0:T(8,128)S(1)} %get-tuple-element.168), channel_id=1, source_target_pairs={{0,1},{1,2},{2,3},{3,0},{4,5},{5,6},{6,7},{7,4},{8,9},{9,10},{10,1... | collective-permute-start | bytes 393224 | tf_op jit(solution)/shard_map/ppermute | solution.py:33
  44.9 5.2 %collective-permute-start.22 = (f32[128,256]{1,0:T(8,128)S(1)}, f32[128,256]{1,0:T(8,128)S(1)}, u32[]{:S(2)}, u32[]{:S(2)}) collective-permute-start(f32[128,256]{1,0:T(8,128)S(1)} %get-tuple-element.170), channel_id=1, source_target_pairs={{0,1},{1,2},{2,3},{3,0},{4,5},{5,6},{6,7},{7,4},{8,9},{9,10},{10,1... | collective-permute-start | bytes 393224 | tf_op jit(solution)/shard_map/ppermute | solution.py:33
  46.3 5.2 %collective-permute-start.23 = (f32[128,256]{1,0:T(8,128)S(1)}, f32[128,256]{1,0:T(8,128)S(1)}, u32[]{:S(2)}, u32[]{:S(2)}) collective-permute-start(f32[128,256]{1,0:T(8,128)S(1)} %get-tuple-element.172), channel_id=1, source_target_pairs={{0,1},{1,2},{2,3},{3,0},{4,5},{5,6},{6,7},{7,4},{8,9},{9,10},{10,1... | collective-permute-start | bytes 393224 | tf_op jit(solution)/shard_map/ppermute | solution.py:33
  47.7 5.2 %collective-permute-start.26 = (f32[128,256]{1,0:T(8,128)S(1)}, f32[128,256]{1,0:T(8,128)S(1)}, u32[]{:S(2)}, u32[]{:S(2)}) collective-permute-start(f32[128,256]{1,0:T(8,128)S(1)} %get-tuple-element.178), channel_id=1, source_target_pairs={{0,1},{1,2},{2,3},{3,0},{4,5},{5,6},{6,7},{7,4},{8,9},{9,10},{10,1... | collective-permute-start | bytes 393224 | tf_op jit(solution)/shard_map/ppermute | solution.py:33
  49.1 5.2 %collective-permute-start.25 = (f32[128,256]{1,0:T(8,128)S(1)}, f32[128,256]{1,0:T(8,128)S(1)}, u32[]{:S(2)}, u32[]{:S(2)}) collective-permute-start(f32[128,256]{1,0:T(8,128)S(1)} %get-tuple-element.177), channel_id=1, source_target_pairs={{0,1},{1,2},{2,3},{3,0},{4,5},{5,6},{6,7},{7,4},{8,9},{9,10},{10,1... | collective-permute-start | bytes 393224 | tf_op jit(solution)/shard_map/ppermute | solution.py:33
  50.5 5.2 %collective-permute-start.24 = (f32[128,256]{1,0:T(8,128)S(1)}, f32[128,256]{1,0:T(8,128)S(1)}, u32[]{:S(2)}, u32[]{:S(2)}) collective-permute-start(f32[128,256]{1,0:T(8,128)S(1)} %get-tuple-element.176), channel_id=1, source_target_pairs={{0,1},{1,2},{2,3},{3,0},{4,5},{5,6},{6,7},{7,4},{8,9},{9,10},{10,1... | collective-permute-start | bytes 393224 | tf_op jit(solution)/shard_map/ppermute | solution.py:33
  51.9 5.2 %collective-permute-start.27 = (f32[128,256]{1,0:T(8,128)S(1)}, f32[128,256]{1,0:T(8,128)S(1)}, u32[]{:S(2)}, u32[]{:S(2)}) collective-permute-start(f32[128,256]{1,0:T(8,128)S(1)} %get-tuple-element.182), channel_id=1, source_target_pairs={{0,1},{1,2},{2,3},{3,0},{4,5},{5,6},{6,7},{7,4},{8,9},{9,10},{10,1... | collective-permute-start | bytes 393224 | tf_op jit(solution)/shard_map/ppermute | solution.py:33
